TPU v7x, 768 devices: a whole 4x8x12 slice. The times are simulated.
768 devices in a mesh: ctx: 96 (over x, z, core), dp: 8 (over y).
Axes of the slice: x: 4, y: 8, z: 12, core: 2. Of those that a mesh axis runs over, the one named last changes fastest.
Arguments:
- queries: bfloat16 [24576, 4096], P('ctx', 'dp'), may hold values from -140 to 140
- keys: bfloat16 [24576, 4096], P('ctx', 'dp'), may hold values from -4.5 to 4.5
- values: bfloat16 [24576, 4096], P('ctx', 'dp'), may hold values from -70 to 70
- doc_ids: int32 [24576], replicated, may hold values from 0 to 7, never falling along the last dimension, each value on 1 to 6144 neighbouring positions
- key_blocks: int32 [192, 6], P('ctx'), may hold values from -1 to 191, as said below
- norm_gain: float32 [4096], P('dp'), may hold values from 0.5 to 1.5
Outputs:
- mixed: bfloat16 [24576, 4096], P('ctx', 'dp')
Inputs may be any that keep to these rules, and one draw needn't show every extreme that they name: `key_blocks`: row b lists 6 different blocks, among them b and b - 6, all of them between b - 6 and b; an entry that would lie before block 0 is -1. `doc_ids`: document numbers never fall along the sequence.
All inputs are finite; a program needn't handle non-finite values.
Results may differ from a plain program's by a relative error of at most 0.0048.
Values may be sent and summed in bfloat16 or wider, within the bound.
No kernel may reach another device: no remote copies, remote signals or barrier semaphores. Data moves between devices by JAX's collectives and lax.ppermute only.
A program may use at most 64 MiB of HBM per device.

v0:
```python
import math

import jax
import jax.numpy as jnp
from jax import lax
from jax.sharding import PartitionSpec as P

HEADS = 32
HD = 128
BLK = 128
NB = 6


def prefix(value, axis, join, neutral):
    count, mine = (lax.axis_size(axis), lax.axis_index(axis))
    pieces = jax.tree.map(lambda part: lax.all_gather(part, axis), value)
    running = jax.tree.map(
        lambda part, zero: jnp.full_like(part, 0) + jnp.asarray(zero, part.dtype), value, neutral
    )

    def hop(position, running):
        longer = join(running, jax.tree.map(lambda part: part[position], pieces))
        return jax.tree.map(lambda new, old: jnp.where(position < mine, new, old), longer, running)

    return lax.fori_loop(0, count - 1, hop, running)


def shifted(x, axis, by):
    devices = lax.axis_size(axis)
    pairs = [(i, i + by) for i in range(devices) if 0 <= i + by < devices]
    return lax.ppermute(x, axis, pairs)


def join_states(earlier, later):
    early_doc, early_state = earlier
    late_doc, late_state = later
    vacant = late_doc < 0.0
    joined_doc = jnp.where(vacant, early_doc, late_doc)
    added = late_state + jnp.where(early_doc == late_doc, early_state, 0.0)
    joined_state = jnp.where(vacant, early_state, added)
    return (joined_doc, joined_state)


def local_blocks(q_blocks, k_blocks, v_blocks, d_blocks, start_doc, start_state):

    def advance(carry, pieces):
        carry_doc, carried = carry
        q_block, k_block, v_block, d_block = pieces
        d_float = d_block.astype(jnp.float32)
        block_last = d_float[-1]
        inner = jnp.einsum(
            "thd,hde->the",
            q_block,
            carried.astype(jnp.bfloat16),
            preferred_element_type=jnp.float32,
        )
        inner = inner * (d_float == carry_doc).astype(jnp.float32)[:, None, None]
        places = jnp.arange(d_block.shape[0])
        allowed = (places[:, None] >= places[None, :]) & (d_block[:, None] == d_block[None, :])
        local_scores = jnp.einsum(
            "thd,shd->hts", q_block, k_block, preferred_element_type=jnp.float32
        )
        local_scores = jnp.where(allowed[None], local_scores, 0.0).astype(jnp.bfloat16)
        intra = jnp.einsum(
            "hts,she->the", local_scores, v_block, preferred_element_type=jnp.float32
        )
        keep_rows = (d_float == block_last).astype(jnp.bfloat16)
        update = jnp.einsum(
            "thd,the->hde",
            k_block,
            v_block * keep_rows[:, None, None],
            preferred_element_type=jnp.float32,
        )
        carried = jnp.where(carry_doc == block_last, carried, 0.0) + update
        return ((block_last, carried), inner + intra)

    _, outputs = lax.scan(
        advance, (start_doc, start_state), (q_blocks, k_blocks, v_blocks, d_blocks)
    )
    return outputs


def local(queries, keys, values, doc_ids, key_blocks, norm_gain):
    tok_rows = queries.shape[0]
    feat_width = queries.shape[1]
    head_count = feat_width // HD
    block_count = tok_rows // BLK
    ctx_place = lax.axis_index("ctx")
    first_row = ctx_place * tok_rows
    docs_here = lax.dynamic_slice_in_dim(doc_ids, first_row, tok_rows)
    k_heads = keys.reshape(tok_rows, head_count, HD)
    v_heads = values.reshape(tok_rows, head_count, HD)
    final_doc = docs_here[-1]
    keep_rows = (docs_here == final_doc).astype(jnp.bfloat16)
    summary = jnp.einsum(
        "thd,the->hde",
        k_heads,
        v_heads * keep_rows[:, None, None],
        preferred_element_type=jnp.float32,
    )
    vacant = (jnp.float32(-1.0), jnp.zeros_like(summary))
    before_doc, before_state = prefix(
        (final_doc.astype(jnp.float32), summary), "ctx", join_states, vacant
    )
    q_blocks = queries.reshape(block_count, BLK, head_count, HD)
    k_blocks = keys.reshape(block_count, BLK, head_count, HD)
    v_blocks = values.reshape(block_count, BLK, head_count, HD)
    d_blocks = docs_here.reshape(block_count, BLK)
    linear_out = local_blocks(q_blocks, k_blocks, v_blocks, d_blocks, before_doc, before_state)
    linear_out = linear_out.reshape(tok_rows, head_count, HD)
    current = (keys, values)
    earlier = []
    for repeat_no in range(3):
        current = shifted((current[0], current[1]), "ctx", 1)
        earlier.insert(0, current)
    window_keys = jnp.concatenate([piece[0] for piece in earlier] + [keys], axis=0)
    window_values = jnp.concatenate([piece[1] for piece in earlier] + [values], axis=0)
    window_keys = window_keys.reshape(4 * block_count, BLK, head_count, HD)
    window_values = window_values.reshape(4 * block_count, BLK, head_count, HD)
    base_block = (ctx_place - 3) * block_count
    present = key_blocks >= 0
    chosen = jnp.where(present, key_blocks, 0)
    slots = jnp.clip(key_blocks - base_block, 0, 4 * block_count - 1)
    key_sel = window_keys[slots].reshape(block_count, NB * BLK, head_count, HD)
    value_sel = window_values[slots].reshape(block_count, NB * BLK, head_count, HD)
    key_pos = (chosen[:, :, None] * BLK + jnp.arange(BLK, dtype=jnp.int32)[None, None, :]).reshape(
        block_count, NB * BLK
    )
    key_doc = doc_ids[key_pos]
    key_live = jnp.repeat(present, BLK, axis=1)
    query_pos = (first_row + jnp.arange(tok_rows, dtype=jnp.int32)).reshape(block_count, BLK)
    allowed = (
        key_live[:, None, :]
        & (key_doc[:, None, :] == d_blocks[:, :, None])
        & (key_pos[:, None, :] <= query_pos[:, :, None])
    )
    scale = 1.0 / math.sqrt(HD)
    scores = (
        jnp.einsum("bthd,bshd->bhts", q_blocks, key_sel, preferred_element_type=jnp.float32) * scale
    )
    scores = jnp.where(allowed[:, None], scores, -jnp.inf)
    top = jnp.max(scores, axis=-1, keepdims=True)
    expo = jnp.exp(scores - top)
    weights = (expo / jnp.sum(expo, axis=-1, keepdims=True)).astype(jnp.bfloat16)
    soft_out = jnp.einsum("bhts,bshe->bthe", weights, value_sel, preferred_element_type=jnp.float32)
    soft_out = soft_out.reshape(tok_rows, feat_width)
    squares = jnp.sum(linear_out * linear_out, axis=(1, 2))
    total = lax.psum(squares, "dp")
    inverse = lax.rsqrt(total / (HEADS * HD) + 1e-06)
    normed = (linear_out * inverse[:, None, None]).reshape(tok_rows, feat_width) * norm_gain
    return (normed + soft_out).astype(jnp.bfloat16)


def solution(mesh):
    return jax.shard_map(
        local,
        mesh=mesh,
        in_specs=(P("ctx", "dp"), P("ctx", "dp"), P("ctx", "dp"), P(), P("ctx", None), P("dp")),
        out_specs=P("ctx", "dp"),
        check_vma=False,
    )
```

profile of v0, /device:TPU:8, one launch (start us, length us, event | category | flops | bytes accessed | tf_op | source)
XLA Modules:
  0.0 629.4 jit_solution(11326070566389658103)
XLA Ops:
  8.0 1.4 compare_convert_fusion.2
  9.4 1.1 copy.92
  10.5 1.2 convolution_bitcast_fusion.1
  12.6 1.8 collective-permute-start.3
  14.3 4.6 collective-permute-start
  19.3 2.9 collective-permute-start.4
  22.2 5.1 collective-permute-start.1
  27.3 8.4 %gather_fusion.1 = s32[1536]{0:T(1024)S(1)} fusion(s32[24576]{0:T(1024)S(1)} %copy-done, s32[2048]{0:T(1024)S(1)} %pad_clamp_fusion), kind=kCustom, calls=%fused_computation.1 | custom fusion | bytes 18432 | tf_op jit(solution)/shard_map/gather | solution.py:129
  35.7 2.1 collective-permute-start.5
  37.9 4.2 collective-permute-start.2
  42.1 1.9 compare_and_fusion
  45.7 1.3 dynamic-slice
  47.8 193.9 %all-reduce = f32[96]{0:T(128)S(1)} all-reduce(f32[96]{0:T(128)S(1)} %dynamic-update-slice), channel_id=1, replica_groups=mesh['ctx'=96,'dp'=8] {'ctx'}, use_global_device_ids=true, to_apply=%add | all-reduce | flops 96 | bytes 768
  243.3 1.3 copy.81
  244.6 1.1 pad_maximum_fusion
  247.2 1.3 copy-done.1
  249.4 1.6 fusion.47
  252.1 345.8 %while.31 = (s32[]{:T(128)}, f32[]{:T(128)}, f32[4,128,128]{2,1,0:T(8,128)S(1)}, s32[]{:T(128)}, f32[96]{0:T(128)S(1)}, /*index=5*/f32[96,4,128,128]{3,2,1,0:T(8,128)}, s32[]{:T(128)}, f32[]{:T(128)}, s32[]{:T(128)}) while((s32[]{:T(128)}, f32[]{:T(128)}, f32[4,128,128]{2,1,0:T(8,128)S(1)}, s32[]{:T(128)}, f32[96]{0:T(128)S(1)}, ...), condition=%wide.region_1.2_spmd.clone, body=%wide.region_0.1_spmd.clone.sunk | while | flops 327688 | bytes 786607 | solution.py:25
  254.0 1.1 select_select_fusion.2
  257.6 1.1 select_select_fusion.2
  261.2 1.1 select_select_fusion.2
  264.9 1.1 select_select_fusion.2
  268.5 1.1 select_select_fusion.2
  272.2 1.1 select_select_fusion.2
  275.8 1.1 select_select_fusion.2
  283.1 1.1 select_select_fusion.2
  286.7 1.1 select_select_fusion.2
  294.0 1.1 select_select_fusion.2
  297.6 1.1 select_select_fusion.2
  304.9 1.1 select_select_fusion.2
  308.6 1.1 select_select_fusion.2
  312.2 1.1 select_select_fusion.2
  315.8 1.1 select_select_fusion.2
  319.5 1.1 select_select_fusion.2
  323.1 1.1 select_select_fusion.2
  326.8 1.1 select_select_fusion.2
  330.4 1.1 select_select_fusion.2
  334.1 1.1 select_select_fusion.2
  337.7 1.1 select_select_fusion.2
  341.3 1.1 select_select_fusion.2
  345.0 1.1 select_select_fusion.2
  352.3 1.1 select_select_fusion.2
  355.9 1.1 select_select_fusion.2
  363.2 1.1 select_select_fusion.2
  366.8 1.1 select_select_fusion.2
  374.1 1.1 select_select_fusion.2
  377.7 1.1 select_select_fusion.2
  381.4 1.1 select_select_fusion.2
  385.0 1.1 select_select_fusion.2
  388.7 1.1 select_select_fusion.2
  392.3 1.1 select_select_fusion.2
  395.9 1.1 select_select_fusion.2
  399.6 1.1 select_select_fusion.2
  403.2 1.1 select_select_fusion.2
  406.9 1.1 select_select_fusion.2
  410.5 1.1 select_select_fusion.2
  414.1 1.1 select_select_fusion.2
  421.4 1.1 select_select_fusion.2
  425.1 1.1 select_select_fusion.2
  432.3 1.1 select_select_fusion.2
  436.0 1.1 select_select_fusion.2
  443.3 1.1 select_select_fusion.2
  597.9 7.1 %while.30 = (s32[]{:T(128)}, f32[]{:T(128)}, f32[4,128,128]{2,1,0:T(8,128)S(1)}, f32[2,128,4,128]{3,1,2,0:T(8,128)S(1)}, s32[2,128]{1,0:T(2,128)S(1)}, /*index=5...) while((s32[]{:T(128)}, f32[]{:T(128)}, ...), condition=%wide.region_3.4_spmd, body=%wide.region_2.3_spmd.sunk | while | flops 67683200 | bytes 3446411 | solution.py:77
  605.5 16.2 %psum.7 = f32[256]{0:T(256)S(1)} all-reduce(f32[256]{0:T(256)S(1)} %bitcast.130), channel_id=1, replica_groups=mesh['ctx'=96,'dp'=8] {'dp'}, use_global_device_ids=true, to_apply=%region_5.6 | all-reduce | flops 256 | bytes 2048 | tf_op jit(solution)/shard_map/psum | solution.py:148
  (249 shorter events, 125.9 us)
Async XLA Ops:
  6.5 12.6 %copy-start = (s32[24576]{0:T(1024)S(1)}, s32[24576]{0:T(1024)}, u32[]{:S(2)}) copy-start(s32[24576]{0:T(1024)} %param.13) | copy-start | bytes 294916
  6.5 7.8 %copy-start.5 = (bf16[256,512]{1,0:T(8,128)(2,1)S(1)}, bf16[256,512]{1,0:T(8,128)(2,1)}, u32[]{:S(2)}) copy-start(bf16[256,512]{1,0:T(8,128)(2,1)} %param.12) | copy-start | bytes 786436
  6.5 6.0 copy-start.7
  6.5 12.4 %copy-start.14 = (s32[2,6]{1,0:T(2,128)S(1)}, s32[2,6]{1,0:T(2,128)}, u32[]{:S(2)}) copy-start(s32[2,6]{1,0:T(2,128)} %param.14) | copy-start | bytes 148
  6.5 245.5 %all-gather.3.cloned.1.call-start = ((), (), s32[]{:S(2)}) async-start(), calls=%async_computation | async-start | bytes 25427968 | tf_op jit(solution)/shard_map/all_gather | solution.py:16
  12.6 6.7 %collective-permute-start.3 = (bf16[256,512]{1,0:T(8,128)(2,1)S(1)}, bf16[256,512]{1,0:T(8,128)(2,1)S(1)}, u32[]{:S(2)}, u32[]{:S(2)}) collective-permute-start(bf16[256,512]{1,0:T(8,128)(2,1)S(1)} %copy-done.7), channel_id=1, source_target_pairs={{0,8},{8,16},{16,24},{24,32},{32,40},{40,48},{48,56},{56,64},{64,7... | collective-permute-start | bytes 786440 | tf_op jit(solution)/shard_map/ppermute | solution.py:31
  14.3 7.8 %collective-permute-start = (bf16[256,512]{1,0:T(8,128)(2,1)S(1)}, bf16[256,512]{1,0:T(8,128)(2,1)S(1)}, u32[]{:S(2)}, u32[]{:S(2)}) collective-permute-start(bf16[256,512]{1,0:T(8,128)(2,1)S(1)} %copy-done.5), channel_id=1, source_target_pairs={{0,8},{8,16},{16,24},{24,32},{32,40},{40,48},{48,56},{56,64},{64,7... | collective-permute-start | bytes 786440 | tf_op jit(solution)/shard_map/ppermute | solution.py:31
  19.3 16.4 %collective-permute-start.4 = (bf16[256,512]{1,0:T(8,128)(2,1)S(1)}, bf16[256,512]{1,0:T(8,128)(2,1)S(1)}, u32[]{:S(2)}, u32[]{:S(2)}) collective-permute-start(bf16[256,512]{1,0:T(8,128)(2,1)S(1)} %collective-permute-done.3), channel_id=1, source_target_pairs={{0,8},{8,16},{16,24},{24,32},{32,40},{40,48},{48,56},{56,64},{64,7... | collective-permute-start | bytes 786440 | tf_op jit(solution)/shard_map/ppermute | solution.py:31
  22.2 13.5 %copy-start.10 = (bf16[256,512]{1,0:T(8,128)(2,1)}, bf16[256,512]{1,0:T(8,128)(2,1)S(1)}, u32[]{:S(2)}) copy-start(bf16[256,512]{1,0:T(8,128)(2,1)S(1)} %collective-permute-done) | copy-start | bytes 786436
  22.2 15.7 %collective-permute-start.1 = (bf16[256,512]{1,0:T(8,128)(2,1)S(1)}, bf16[256,512]{1,0:T(8,128)(2,1)}, u32[]{:S(2)}, u32[]{:S(2)}) collective-permute-start(bf16[256,512]{1,0:T(8,128)(2,1)S(1)} %collective-permute-done), channel_id=1, source_target_pairs={{0,8},{8,16},{16,24},{24,32},{32,40},{40,48},{48,56},{56,64},{64,7... | collective-permute-start | bytes 786440 | tf_op jit(solution)/shard_map/ppermute | solution.py:31
  27.3 18.3 %copy-start.9 = (bf16[256,512]{1,0:T(8,128)(2,1)S(1)}, bf16[256,512]{1,0:T(8,128)(2,1)}, u32[]{:S(2)}) copy-start(bf16[256,512]{1,0:T(8,128)(2,1)} %param.10) | copy-start | bytes 786436
  35.7 206.0 %collective-permute-start.5 = (bf16[256,512]{1,0:T(8,128)(2,1)S(1)}, bf16[256,512]{1,0:T(8,128)(2,1)S(1)}, u32[]{:S(2)}, u32[]{:S(2)}) collective-permute-start(bf16[256,512]{1,0:T(8,128)(2,1)S(1)} %collective-permute-done.4), channel_id=1, source_target_pairs={{0,8},{8,16},{16,24},{24,32},{32,40},{40,48},{48,56},{56,64},{64,7... | collective-permute-start | bytes 786440 | tf_op jit(solution)/shard_map/ppermute | solution.py:31
  37.9 206.7 %collective-permute-start.2 = (bf16[256,512]{1,0:T(8,128)(2,1)}, bf16[256,512]{1,0:T(8,128)(2,1)}, u32[]{:S(2)}, u32[]{:S(2)}) collective-permute-start(bf16[256,512]{1,0:T(8,128)(2,1)} %collective-permute-done.1), channel_id=1, source_target_pairs={{0,8},{8,16},{16,24},{24,32},{32,40},{40,48},{48,56},{56,64},{64,7... | collective-permute-start | bytes 786440 | tf_op jit(solution)/shard_map/ppermute | solution.py:31
  45.6 196.1 %copy-start.3 = (bf16[2,128,4,128]{3,2,1,0:T(4,128)(2,1)}, bf16[2,128,4,128]{3,2,1,0:T(4,128)(2,1)S(1)}, u32[]{:S(2)}) copy-start(bf16[2,128,4,128]{3,2,1,0:T(4,128)(2,1)S(1)} %reshape.186) | copy-start | bytes 786436
  243.2 1.3 copy-start.6
  243.2 1.3 copy-start.11
  247.1 1.4 copy-start.1
  247.1 1.4 copy-start.4
  248.5 0.9 copy-start.12
  252.0 345.9 %copy-start.2 = (bf16[2,128,4,128]{3,2,1,0:T(4,128)(2,1)S(1)}, bf16[2,128,4,128]{3,2,1,0:T(4,128)(2,1)}, u32[]{:S(2)}) copy-start(bf16[2,128,4,128]{3,2,1,0:T(4,128)(2,1)} %reshape.185) | copy-start | bytes 786436
  252.0 345.9 %copy-start.8 = (f32[2,128,4,128]{3,1,2,0:T(8,128)S(1)}, f32[2,128,4,128]{3,1,2,0:T(8,128)}, u32[]{:S(2)}) copy-start(f32[2,128,4,128]{3,1,2,0:T(8,128)} %custom-call.7) | copy-start | bytes 1572868
  597.9 23.8 %copy-start.13 = (f32[512]{0:T(512)S(1)}, f32[512]{0:T(512)}, u32[]{:S(2)}) copy-start(f32[512]{0:T(512)} %param.15) | copy-start | bytes 6148
Sparse Core Ops, SparseCore 0:
  12.7 161.9 all-gather.2
where the time goes:
time: 636 us; the launch traced here: 629 us
  blocking collectives  210 us (33%)
  loops' own time  190 us (30%)
  other arithmetic  111 us (17%)
  local copies, waits for them, and re-layouts  79.2 us (12%)
  starting transfers between devices  20.6 us (3%)
  between operations  14.5 us (2%)
    unnamed x1, blocking collectives  194 us
    another operation x1, loops' own time, prefix(): return lax.fori_loop(0, count - 1, hop, running)  188 us
    select_n x95, other arithmetic, hop(): jnp.where(position < mine, new, old)  102 us
    dynamic_slice x95, local copies, waits for them, and re-layouts, hop(): longer = join(running, jax.tree.map(lambda part: part[position], pieces))  55.7 us
    ppermute x6, starting transfers between devices, shifted(): return lax.ppermute(x, axis, pairs)  20.6 us
    psum x1, blocking collectives, local(): total = lax.psum(squares, 'dp')  16.2 us
  transfers between devices with their start and end apart: 7, of which 0 were waited for; matrix products, arithmetic and copies ran while one was open for 4% of the time, Pallas kernels for 0%

commit v1 on v0

v1 whole, which is shorter than its diff:
```python
import functools
import math

import jax
import jax.numpy as jnp
from jax import lax
from jax.experimental import pallas as pl
from jax.experimental.pallas import tpu as pltpu
from jax.sharding import PartitionSpec as P

HEADS = 32
HD = 128
BLK = 128
NB = 6
ROW = 24
PIECE = 24
NEG = -1e30
F32 = jnp.float32
BF16 = jnp.bfloat16
VM = pl.BlockSpec(memory_space=pltpu.VMEM)
SM = pl.BlockSpec(memory_space=pltpu.SMEM)


def call(body, outs, ins, name):
    return pl.pallas_call(
        body,
        out_shape=outs,
        in_specs=ins,
        out_specs=jax.tree.map(lambda _: VM, outs),
        name=name,
    )


def dot_nn(a, b):
    return lax.dot_general(a, b, (((1,), (0,)), ((), ())), preferred_element_type=F32)


def dot_nt(a, b):
    return lax.dot_general(a, b, (((1,), (1,)), ((), ())), preferred_element_type=F32)


def dot_tn(a, b):
    return lax.dot_general(a, b, (((0,), (0,)), ((), ())), preferred_element_type=F32)


def doc_row(doc_ref, row):
    return doc_ref[pl.ds(row, 1), :].astype(F32)


def down(row):
    return jnp.broadcast_to(row, (BLK, BLK)).T


def count_below(row, value):
    return jnp.sum(jnp.where(row < value, 1.0, 0.0), axis=1, keepdims=True)


def head(h):
    return slice(h * HD, (h + 1) * HD)


def summary_kernel(doc_ref, k_ref, v_ref, state_ref, kv_ref):
    me = lax.axis_index("ctx")
    d0, d1 = doc_row(doc_ref, 2 * me), doc_row(doc_ref, 2 * me + 1)
    last = d1[:, BLK - 1 :]
    first = count_below(d0, last) + count_below(d1, last)
    rows = lax.broadcasted_iota(jnp.int32, (2 * BLK, HD), 0).astype(F32)
    keep = rows >= first
    for h in range(4):
        vm = jnp.where(keep, v_ref[:, head(h)].astype(F32), 0.0).astype(BF16)
        state_ref[head(h), :] = dot_tn(k_ref[:, head(h)], vm).astype(BF16)
    state_ref[4 * HD :, :] = jnp.zeros((ROW * PIECE - 4 * HD, HD), BF16)
    kv_ref[: 2 * BLK, :] = k_ref[...]
    kv_ref[2 * BLK :, :] = v_ref[...]


def row_docs(doc_ref):
    row = lax.axis_index("ctx") // ROW
    docs = doc_ref[pl.ds(pl.multiple_of(row * 2 * ROW, 8), 2 * ROW), :].astype(F32)
    return row, jnp.broadcast_to(docs[:, BLK - 1 :], (2 * ROW, HD))


def total_kernel(doc_ref, piece_ref, total_ref):
    _, docs = row_docs(doc_ref)
    last = docs[2 * ROW - 1 :, :]
    total = jnp.zeros((PIECE, HD), F32)
    for j in range(ROW):
        same = docs[2 * j + 1 : 2 * j + 2, :] == last
        total += jnp.where(same, piece_ref[j].astype(F32), 0.0)
    total_ref[...] = total


def prefix_kernel(doc_ref, piece_ref, carry_ref, before_ref):
    row, docs = row_docs(doc_ref)
    past = doc_row(doc_ref, jnp.maximum(2 * ROW * row - 1, 0))
    before = jnp.broadcast_to(past[:, BLK - 1 :], (1, HD))
    running = carry_ref[...]
    for j in range(ROW):
        before_ref[j] = running.astype(BF16)
        now = docs[2 * j + 1 : 2 * j + 2, :]
        running = jnp.where(now == before, running, 0.0) + piece_ref[j].astype(F32)
        before = now


def linear_kernel(doc_ref, q_ref, k_ref, v_ref, state_ref, lin_ref, sq_ref):
    me = lax.axis_index("ctx")
    past = doc_row(doc_ref, jnp.maximum(2 * me - 1, 0))[:, BLK - 1 :]
    lane = lax.broadcasted_iota(jnp.int32, (BLK, BLK), 1)
    line = lax.broadcasted_iota(jnp.int32, (BLK, BLK), 0)
    causal = lane <= line
    docs = [doc_row(doc_ref, 2 * me), doc_row(doc_ref, 2 * me + 1)]
    lasts = [docs[0][:, BLK - 1 :], docs[1][:, BLK - 1 :]]
    cols = [down(docs[0]), down(docs[1])]
    keep = cols[0] == lasts[0]
    squares = [jnp.zeros((BLK, HD), F32), jnp.zeros((BLK, HD), F32)]
    for h in range(4):
        state = state_ref[head(h), :]
        for t in range(2):
            rows = slice(t * BLK, (t + 1) * BLK)
            q, k, v = q_ref[rows, head(h)], k_ref[rows, head(h)], v_ref[rows, head(h)]
            inner = jnp.where(cols[t] == past if t == 0 else cols[t] == lasts[0], dot_nn(q, state), 0.0)
            scores = jnp.where(causal & (cols[t] == docs[t]), dot_nt(q, k), 0.0).astype(BF16)
            lin = inner + dot_nn(scores, v)
            lin_ref[rows, head(h)] = lin
            squares[t] += lin * lin
            if t == 0:
                update = dot_tn(k, jnp.where(keep, v.astype(F32), 0.0).astype(BF16))
                state = (jnp.where(past == lasts[0], state.astype(F32), 0.0) + update).astype(BF16)
    sums = [jnp.sum(square.T, axis=0, keepdims=True) for square in squares]
    row = lax.broadcasted_iota(jnp.int32, (8, BLK), 0)
    tile = jnp.where(row == 0, sums[0], jnp.where(row == 1, sums[1], 0.0))
    for place in range(sq_ref.shape[0]):
        sq_ref[place] = tile


def soft_kernel(list_ref, doc_ref, q_ref, kv0_ref, kv1_ref, kv2_ref, kv3_ref, soft_ref):
    me = lax.axis_index("ctx")
    base = 2 * me - NB
    lane = lax.broadcasted_iota(jnp.int32, (BLK, BLK), 1)
    line = lax.broadcasted_iota(jnp.int32, (BLK, BLK), 0)
    causal = lane <= line
    docs = [doc_row(doc_ref, jnp.maximum(base + w, 0)) for w in range(8)]
    scale = 1.0 / math.sqrt(HD)
    allowed = []
    for t in range(2):
        col = down(docs[NB + t])
        for w in range(8):
            if w < t or w > NB + t:
                allowed.append(None)
                continue
            block = base + w
            listed = list_ref[t, 0] == block
            for n in range(1, NB):
                listed = listed | (list_ref[t, n] == block)
            listed = listed & (block >= 0)
            match = col == jnp.where(listed, docs[w], -1.0)
            allowed.append(match & causal if w == NB + t else match)
    kvs = [kv3_ref, kv2_ref, kv1_ref, kv0_ref]
    for h in range(4):
        q = q_ref[:, head(h)]
        raw = [dot_nt(q, kv[: 2 * BLK, head(h)]) for kv in kvs]
        weights = [[], []]
        for t in range(2):
            rows = slice(t * BLK, (t + 1) * BLK)
            pieces = []
            for w in range(8):
                mask = allowed[8 * t + w]
                if mask is None:
                    pieces.append(None)
                    continue
                piece = raw[w // 2][rows, (w % 2) * BLK : (w % 2 + 1) * BLK]
                pieces.append(jnp.where(mask, piece, NEG))
            live = [piece for piece in pieces if piece is not None]
            top = jnp.max(functools.reduce(jnp.maximum, live), axis=1, keepdims=True)
            expos = [None if piece is None else jnp.exp((piece - top) * scale) for piece in pieces]
            total = jnp.sum(sum(e for e in expos if e is not None), axis=1, keepdims=True)
            share = 1.0 / total
            weights[t] = [
                jnp.zeros((BLK, BLK), BF16) if e is None else (e * share).astype(BF16) for e in expos
            ]
        out = jnp.zeros((2 * BLK, HD), F32)
        for d in range(4):
            both = jnp.concatenate(
                [jnp.concatenate([weights[t][2 * d], weights[t][2 * d + 1]], axis=1) for t in range(2)],
                axis=0,
            )
            out += dot_nn(both, kvs[d][2 * BLK :, head(h)])
        soft_ref[:, head(h)] = out


def mix_kernel(lin_ref, soft_ref, sq_ref, gain_ref, out_ref):
    total = jnp.sum(sq_ref[...], axis=0)
    inverse = lax.rsqrt(total / (HEADS * HD) + 1e-06)
    for t in range(2):
        rows = slice(t * BLK, (t + 1) * BLK)
        col = down(inverse[t : t + 1, :])
        for h in range(4):
            normed = lin_ref[rows, head(h)] * col * gain_ref[:, head(h)]
            out_ref[rows, head(h)] = (normed + soft_ref[rows, head(h)]).astype(BF16)


def local(queries, keys, values, doc_ids, key_blocks, norm_gain):
    tok_rows, feat_width = queries.shape
    devices = lax.axis_size("ctx")
    parts = lax.axis_size("dp")
    docs = doc_ids.reshape(-1, BLK)
    gain = norm_gain.reshape(1, feat_width)
    shape = jax.ShapeDtypeStruct
    groups = [list(range(first, first + ROW)) for first in range(0, devices, ROW)]

    def shifted(x, by):
        return lax.ppermute(x, "ctx", [(i, i + by) for i in range(devices - by)])

    def exchange(x):
        return lax.all_to_all(x, "ctx", 0, 0, axis_index_groups=groups)

    summary, kv = call(
        summary_kernel,
        (shape((ROW * PIECE, HD), BF16), shape((2 * tok_rows, feat_width), BF16)),
        [VM, VM, VM],
        "summary",
    )(docs, keys, values)
    kv1 = shifted(kv, 1)
    pieces = exchange(summary.reshape(ROW, PIECE, HD))
    kv2 = shifted(kv1, 1)
    total = call(total_kernel, shape((PIECE, HD), F32), [VM, VM], "total")(docs, pieces)
    carry = shifted(total, ROW)
    before = call(prefix_kernel, shape((ROW, PIECE, HD), BF16), [VM, VM, VM], "prefix")(
        docs, pieces, carry
    )
    kv3 = shifted(kv2, 1)
    state = exchange(before).reshape(ROW * PIECE, HD)
    lin, squares = call(
        linear_kernel,
        (shape((tok_rows, feat_width), F32), shape((parts, 8, BLK), F32)),
        [VM] * 5,
        "linear",
    )(docs, queries, keys, values, state)
    squares = lax.all_to_all(squares, "dp", 0, 0)
    soft = call(soft_kernel, shape((tok_rows, feat_width), F32), [SM] + [VM] * 6, "soft")(
        key_blocks, docs, queries, kv, kv1, kv2, kv3
    )
    return call(mix_kernel, shape((tok_rows, feat_width), BF16), [VM] * 4, "mix")(
        lin, soft, squares, gain
    )


def solution(mesh):
    return jax.shard_map(
        local,
        mesh=mesh,
        in_specs=(P("ctx", "dp"), P("ctx", "dp"), P("ctx", "dp"), P(), P("ctx", None), P("dp")),
        out_specs=P("ctx", "dp"),
        check_vma=False,
    )
```

time: 636 us -> 96.1 us (0.15)
  the two profiles are of different devices: /device:TPU:8 before, /device:TPU:2 now
where the time goes in v1:
time: 96.1 us; the launch traced here: 95.6 us
  waiting for transfers between devices  35.7 us (37%)
  starting transfers between devices  23.6 us (25%)
  blocking collectives  17.5 us (18%)
  Pallas kernels  15.9 us (17%)
  local copies, waits for them, and re-layouts  2.67 us (3%)
    ppermute x4, waiting for transfers between devices, shifted(): return lax.ppermute(x, 'ctx', [(i, i + by) for i in range(devices - by)])  24.8 us
    all_to_all x1, blocking collectives, exchange(): return lax.all_to_all(x, 'ctx', 0, 0, axis_index_groups=groups)  17.5 us
    ppermute x4, starting transfers between devices, shifted(): return lax.ppermute(x, 'ctx', [(i, i + by) for i in range(devices - by)])  9.11 us
    all_to_all x1, waiting for transfers between devices, exchange(): return lax.all_to_all(x, 'ctx', 0, 0, axis_index_groups=groups)  8.89 us
    all_to_all x1, starting transfers between devices, exchange(): return lax.all_to_all(x, 'ctx', 0, 0, axis_index_groups=groups)  7.42 us
    all_to_all x1, starting transfers between devices, local(): squares = lax.all_to_all(squares, 'dp', 0, 0)  7.1 us
    pallas_call x1, Pallas kernels, local(): call(soft_kernel, shape((tok_rows, feat_width), F32), [SM] + [VM] * 6, 's...  5.14 us
    pallas_call x1, Pallas kernels, local(): call(linear_kernel, (shape((tok_rows, feat_width), F32), shape((parts, 8,...  3.08 us
  transfers between devices with their start and end apart: 6, of which 5 were waited for; matrix products, arithmetic and copies ran while one was open for 0% of the time, Pallas kernels for 12%

profile of v1, /device:TPU:2, one launch (start us, length us, event | category | flops | bytes accessed | tf_op | source)
XLA Modules:
  0.0 95.6 jit_solution(1336754703651636653)
XLA Ops:
  0.0 2.2 %summary.1 = (bf16[576,128]{1,0:T(8,128)(2,1)}, bf16[512,512]{1,0:T(8,128)(2,1)}) custom-call(s32[192,128]{1,0:T(8,128)} %bitcast.4, bf16[256,512]{1,0:T(8,128)(2,1)} %k_ref.3, bf16[256,512]{1,0:T(8,128)(2,1)} %v_ref.3), custom_call_target="tpu_custom_call" | custom-call | tf_op jit(solution)/shard_map/summary/pallas_call | solution.py:217
  2.2 1.9 %collective-permute-start.1 = (bf16[512,512]{1,0:T(8,128)(2,1)}, bf16[512,512]{1,0:T(8,128)(2,1)S(1)}, u32[]{:S(2)}, u32[]{:S(2)}) collective-permute-start(bf16[512,512]{1,0:T(8,128)(2,1)} %get-tuple-element.11.kv0_ref), channel_id=1, source_target_pairs={{0,8},{8,16},{16,24},{24,32},{32,40},{40,48},{48,56},{56,64},{64,7... | collective-permute-start | bytes 1572872 | tf_op jit(solution)/shard_map/ppermute | solution.py:212
  4.2 19.1 %collective-permute-done.1.kv1_ref = bf16[512,512]{1,0:T(8,128)(2,1)S(1)} collective-permute-done((bf16[512,512]{1,0:T(8,128)(2,1)}, bf16[512,512]{1,0:T(8,128)(2,1)S(1)}, u32[]{:S(2)}, u32[]{:S(2)}) %collective-permute-start.1) | collective-permute-done | bytes 524320 | tf_op jit(solution)/shard_map/ppermute | solution.py:212
  23.3 0.0 copy-start.1
  23.3 1.9 %collective-permute-start.2 = (bf16[512,512]{1,0:T(8,128)(2,1)S(1)}, bf16[512,512]{1,0:T(8,128)(2,1)S(1)}, u32[]{:S(2)}, u32[]{:S(2)}) collective-permute-start(bf16[512,512]{1,0:T(8,128)(2,1)S(1)} %collective-permute-done.1.kv1_ref), channel_id=1, source_target_pairs={{0,8},{8,16},{16,24},{24,32},{32,40},{40,48},{48,56},{56,64},{64,7... | collective-permute-start | bytes 1572872 | tf_op jit(solution)/shard_map/ppermute | solution.py:212
  25.2 7.4 %all-to-all-start = ((bf16[24,24,128]{2,1,0:T(8,128)(2,1)}), bf16[24,24,128]{2,1,0:T(8,128)(2,1)S(1)}, u32[]{:S(2)}, u32[]{:S(2)}) async-start(bf16[24,24,128]{2,1,0:T(8,128)(2,1)} %bitcast.10), calls=%async_computation | async-start | bytes 294912 | tf_op jit(solution)/shard_map/all_to_all | solution.py:215
  32.6 3.3 %collective-permute-done.2.kv2_ref = bf16[512,512]{1,0:T(8,128)(2,1)S(1)} collective-permute-done((bf16[512,512]{1,0:T(8,128)(2,1)S(1)}, bf16[512,512]{1,0:T(8,128)(2,1)S(1)}, u32[]{:S(2)}, u32[]{:S(2)}) %collective-permute-start.2) | collective-permute-done | bytes 524320 | tf_op jit(solution)/shard_map/ppermute | solution.py:212
  35.9 0.0 copy-start.2
  35.9 1.9 %collective-permute-start.3 = (bf16[512,512]{1,0:T(8,128)(2,1)S(1)}, bf16[512,512]{1,0:T(8,128)(2,1)S(1)}, u32[]{:S(2)}, u32[]{:S(2)}) collective-permute-start(bf16[512,512]{1,0:T(8,128)(2,1)S(1)} %collective-permute-done.2.kv2_ref), channel_id=1, source_target_pairs={{0,8},{8,16},{16,24},{24,32},{32,40},{40,48},{48,56},{56,64},{64,7... | collective-permute-start | bytes 1572872 | tf_op jit(solution)/shard_map/ppermute | solution.py:212
  37.8 8.9 %all-to-all-done.piece_ref = bf16[24,24,128]{2,1,0:T(8,128)(2,1)S(1)} async-done(((bf16[24,24,128]{2,1,0:T(8,128)(2,1)}), bf16[24,24,128]{2,1,0:T(8,128)(2,1)S(1)}, u32[]{:S(2)}, u32[]{:S(2)}) %all-to-all-start) | async-done | bytes 147488 | tf_op jit(solution)/shard_map/all_to_all | solution.py:215
  46.7 0.0 copy-start
  46.7 0.7 copy-done
  47.4 1.7 %total.1 = f32[24,128]{1,0:T(8,128)} custom-call(s32[192,128]{1,0:T(8,128)} %bitcast.5, bf16[24,24,128]{2,1,0:T(8,128)(2,1)} %copy-done), custom_call_target="tpu_custom_call" | custom-call | tf_op jit(solution)/shard_map/total/pallas_call | solution.py:226
  49.0 3.4 %collective-permute-start = (f32[24,128]{1,0:T(8,128)}, f32[24,128]{1,0:T(8,128)S(1)}, u32[]{:S(2)}, u32[]{:S(2)}) collective-permute-start(f32[24,128]{1,0:T(8,128)} %total.1), channel_id=1, source_target_pairs={{0,192},{8,200},{16,208},{24,216},{32,224},{40,232},{48,240},{56,2... | collective-permute-start | bytes 36872 | tf_op jit(solution)/shard_map/ppermute | solution.py:212
  52.4 2.4 %collective-permute-done.carry_ref = f32[24,128]{1,0:T(8,128)S(1)} collective-permute-done((f32[24,128]{1,0:T(8,128)}, f32[24,128]{1,0:T(8,128)S(1)}, u32[]{:S(2)}, u32[]{:S(2)}) %collective-permute-start) | collective-permute-done | bytes 12320 | tf_op jit(solution)/shard_map/ppermute | solution.py:212
  54.8 0.0 copy-start.5
  54.8 0.6 copy-done.5
  55.4 1.7 %prefix.1 = bf16[24,24,128]{2,1,0:T(8,128)(2,1)} custom-call(s32[192,128]{1,0:T(8,128)} %bitcast.6, bf16[24,24,128]{2,1,0:T(8,128)(2,1)} %copy-done, f32[24,128]{1,0:T(8,128)} %copy-done.5), custom_call_target="tpu_custom_call" | custom-call | tf_op jit(solution)/shard_map/prefix/pallas_call | solution.py:228
  57.2 17.5 %all_to_all.15 = bf16[24,24,128]{2,1,0:T(8,128)(2,1)} all-to-all(bf16[24,24,128]{2,1,0:T(8,128)(2,1)} %prefix.1), channel_id=1, replica_groups={{0,8,16,24,32,40,48,56,64,72,80,88,96,104,112,120,128,136,144,152,160,1..., dimensions={0} | all-to-all | bytes 294912 | tf_op jit(solution)/shard_map/all_to_all | solution.py:215
  74.7 3.1 %linear.1 = (f32[256,512]{1,0:T(8,128)}, f32[8,8,128]{2,1,0:T(8,128)}) custom-call(s32[192,128]{1,0:T(8,128)} %bitcast.7, bf16[256,512]{1,0:T(8,128)(2,1)} %q_ref.3, bf16[256,512]{1,0:T(8,128)(2,1)} %k_ref.3, bf16[256,512]{1,0:T(8,128)(2,1)} %v_ref.3, bf16[576,128]{1,0:T(8,128)(2,1)} %bitcast.9), custom_call_target="tpu_custom_call" | custom-call | tf_op jit(solution)/shard_map/linear/pallas_call | solution.py:233
  77.8 7.1 %all-to-all-start.2 = ((f32[8,8,128]{2,1,0:T(8,128)}), f32[8,8,128]{2,1,0:T(8,128)S(1)}, u32[]{:S(2)}, u32[]{:S(2)}) async-start(f32[8,8,128]{2,1,0:T(8,128)} %get-tuple-element.12), calls=%async_computation.2 | async-start | bytes 65536 | tf_op jit(solution)/shard_map/all_to_all | solution.py:239
  84.9 0.0 collective-permute-done.3.kv3_ref
  84.9 0.0 copy-done.1
  84.9 0.0 copy-done.2
  84.9 0.0 copy-start.3
  84.9 0.8 copy-done.3
  85.7 5.1 %soft.1.soft_ref = f32[256,512]{1,0:T(8,128)} custom-call(s32[2,6]{1,0:T(2,128)} %list_ref.1, s32[192,128]{1,0:T(8,128)} %bitcast.8, bf16[256,512]{1,0:T(8,128)(2,1)} %q_ref.3, bf16[512,512]{1,0:T(8,128)(2,1)} %get-tuple-element.11.kv0_ref, bf16[512,512]{1,0:T(8,128)(2,1)} %copy-done.1, bf16[512,512]{1,0:T(8,128)(2,1)} %copy-done.2, bf16[512,512]{1,0:T(8,128)(2,1)} %copy-done.3), custom_call_target="tpu_custom_call" | custom-call | tf_op jit(solution)/shard_map/soft/pallas_call | solution.py:240
  90.9 2.0 %all-to-all-done.2.sq_ref = f32[8,8,128]{2,1,0:T(8,128)S(1)} async-done(((f32[8,8,128]{2,1,0:T(8,128)}), f32[8,8,128]{2,1,0:T(8,128)S(1)}, u32[]{:S(2)}, u32[]{:S(2)}) %all-to-all-start.2) | async-done | bytes 32800 | tf_op jit(solution)/shard_map/all_to_all | solution.py:239
  92.9 0.0 copy-start.4
  92.9 0.6 copy-done.4
  93.5 2.1 %mix.1 = bf16[256,512]{1,0:T(8,128)(2,1)} custom-call(f32[256,512]{1,0:T(8,128)} %get-tuple-element.10.lin_ref, f32[256,512]{1,0:T(8,128)} %soft.1.soft_ref, f32[8,8,128]{2,1,0:T(8,128)} %copy-done.4, f32[1,512]{1,0:T(1,128)} %bitcast.11), custom_call_target="tpu_custom_call" | custom-call | tf_op jit(solution)/shard_map/mix/pallas_call | solution.py:243
Async XLA Ops:
  2.2 21.1 %collective-permute-start.1 = (bf16[512,512]{1,0:T(8,128)(2,1)}, bf16[512,512]{1,0:T(8,128)(2,1)S(1)}, u32[]{:S(2)}, u32[]{:S(2)}) collective-permute-start(bf16[512,512]{1,0:T(8,128)(2,1)} %get-tuple-element.11.kv0_ref), channel_id=1, source_target_pairs={{0,8},{8,16},{16,24},{24,32},{32,40},{40,48},{48,56},{56,64},{64,7... | collective-permute-start | bytes 1572872 | tf_op jit(solution)/shard_map/ppermute | solution.py:212
  23.3 61.6 %copy-start.1 = (bf16[512,512]{1,0:T(8,128)(2,1)}, bf16[512,512]{1,0:T(8,128)(2,1)S(1)}, u32[]{:S(2)}) copy-start(bf16[512,512]{1,0:T(8,128)(2,1)S(1)} %collective-permute-done.1.kv1_ref) | copy-start | bytes 1572868
  23.3 12.6 %collective-permute-start.2 = (bf16[512,512]{1,0:T(8,128)(2,1)S(1)}, bf16[512,512]{1,0:T(8,128)(2,1)S(1)}, u32[]{:S(2)}, u32[]{:S(2)}) collective-permute-start(bf16[512,512]{1,0:T(8,128)(2,1)S(1)} %collective-permute-done.1.kv1_ref), channel_id=1, source_target_pairs={{0,8},{8,16},{16,24},{24,32},{32,40},{40,48},{48,56},{56,64},{64,7... | collective-permute-start | bytes 1572872 | tf_op jit(solution)/shard_map/ppermute | solution.py:212
  25.2 21.5 %all-to-all-start = ((bf16[24,24,128]{2,1,0:T(8,128)(2,1)}), bf16[24,24,128]{2,1,0:T(8,128)(2,1)S(1)}, u32[]{:S(2)}, u32[]{:S(2)}) async-start(bf16[24,24,128]{2,1,0:T(8,128)(2,1)} %bitcast.10), calls=%async_computation | async-start | bytes 294912 | tf_op jit(solution)/shard_map/all_to_all | solution.py:215
  35.9 49.0 %copy-start.2 = (bf16[512,512]{1,0:T(8,128)(2,1)}, bf16[512,512]{1,0:T(8,128)(2,1)S(1)}, u32[]{:S(2)}) copy-start(bf16[512,512]{1,0:T(8,128)(2,1)S(1)} %collective-permute-done.2.kv2_ref) | copy-start | bytes 1572868
  35.9 49.0 %collective-permute-start.3 = (bf16[512,512]{1,0:T(8,128)(2,1)S(1)}, bf16[512,512]{1,0:T(8,128)(2,1)S(1)}, u32[]{:S(2)}, u32[]{:S(2)}) collective-permute-start(bf16[512,512]{1,0:T(8,128)(2,1)S(1)} %collective-permute-done.2.kv2_ref), channel_id=1, source_target_pairs={{0,8},{8,16},{16,24},{24,32},{32,40},{40,48},{48,56},{56,64},{64,7... | collective-permute-start | bytes 1572872 | tf_op jit(solution)/shard_map/ppermute | solution.py:212
  46.7 0.7 copy-start
  49.0 5.8 %collective-permute-start = (f32[24,128]{1,0:T(8,128)}, f32[24,128]{1,0:T(8,128)S(1)}, u32[]{:S(2)}, u32[]{:S(2)}) collective-permute-start(f32[24,128]{1,0:T(8,128)} %total.1), channel_id=1, source_target_pairs={{0,192},{8,200},{16,208},{24,216},{32,224},{40,232},{48,240},{56,2... | collective-permute-start | bytes 36872 | tf_op jit(solution)/shard_map/ppermute | solution.py:212
  54.8 0.6 copy-start.5
  77.8 15.1 %all-to-all-start.2 = ((f32[8,8,128]{2,1,0:T(8,128)}), f32[8,8,128]{2,1,0:T(8,128)S(1)}, u32[]{:S(2)}, u32[]{:S(2)}) async-start(f32[8,8,128]{2,1,0:T(8,128)} %get-tuple-element.12), calls=%async_computation.2 | async-start | bytes 65536 | tf_op jit(solution)/shard_map/all_to_all | solution.py:239
  84.9 0.8 copy-start.3
  92.9 0.6 copy-start.4

commit v2 on v1

v2 whole, which is shorter than its diff:
```python
import functools
import math

import jax
import jax.numpy as jnp
from jax import lax
from jax.experimental import pallas as pl
from jax.experimental.pallas import tpu as pltpu
from jax.sharding import PartitionSpec as P


HEADS = 32
HD = 128
BLK = 128
NB = 6
ROW = 24
PIECE = 24
NEG = -1e30
F32 = jnp.float32
BF16 = jnp.bfloat16
VM = pl.BlockSpec(memory_space=pltpu.VMEM)
SM = pl.BlockSpec(memory_space=pltpu.SMEM)


def call(body, outs, *operands):
    smem = [x.shape == (2, NB) for x in operands]
    operands = [
        x if small else pltpu.with_memory_space_constraint(x, pltpu.VMEM)
        for x, small in zip(operands, smem)
    ]
    return pl.pallas_call(
        body,
        out_shape=outs,
        in_specs=[SM if small else VM for small in smem],
        out_specs=jax.tree.map(lambda _: VM, outs),
        compiler_params=pltpu.CompilerParams(vmem_limit_bytes=12 << 20),
    )(*operands)


def dot_nn(a, b):
    return lax.dot_general(a, b, (((1,), (0,)), ((), ())), preferred_element_type=F32)


def dot_nt(a, b):
    return lax.dot_general(a, b, (((1,), (1,)), ((), ())), preferred_element_type=F32)


def dot_tn(a, b):
    return lax.dot_general(a, b, (((0,), (0,)), ((), ())), preferred_element_type=F32)


def doc_row(doc_ref, row):
    return doc_ref[pl.ds(row, 1), :].astype(F32)


def down(row):
    return jnp.broadcast_to(row, (BLK, BLK)).T


def count_below(row, value):
    return jnp.sum(jnp.where(row < value, 1.0, 0.0), axis=1, keepdims=True)


def head(h):
    return slice(h * HD, (h + 1) * HD)


def summary_kernel(doc_ref, k_ref, v_ref, state_ref, kv_ref):
    me = lax.axis_index("ctx")
    d0, d1 = doc_row(doc_ref, 2 * me), doc_row(doc_ref, 2 * me + 1)
    last = d1[:, BLK - 1 :]
    first = count_below(d0, last) + count_below(d1, last)
    rows = lax.broadcasted_iota(jnp.int32, (2 * BLK, HD), 0).astype(F32)
    keep = rows >= first
    for h in range(4):
        vm = jnp.where(keep, v_ref[:, head(h)].astype(F32), 0.0).astype(BF16)
        state_ref[head(h), :] = dot_tn(k_ref[:, head(h)], vm).astype(BF16)
    state_ref[4 * HD :, :] = jnp.zeros((ROW * PIECE - 4 * HD, HD), BF16)
    kv_ref[: 2 * BLK, :] = k_ref[...]
    kv_ref[2 * BLK :, :] = v_ref[...]


def row_docs(doc_ref):
    row = lax.axis_index("ctx") // ROW
    docs = doc_ref[pl.ds(pl.multiple_of(row * 2 * ROW, 8), 2 * ROW), :].astype(F32)
    return row, jnp.broadcast_to(docs[:, BLK - 1 :], (2 * ROW, HD))


def total_kernel(doc_ref, piece_ref, total_ref):
    _, docs = row_docs(doc_ref)
    last = docs[2 * ROW - 1 :, :]
    total = jnp.zeros((PIECE, HD), F32)
    for j in range(ROW):
        same = docs[2 * j + 1 : 2 * j + 2, :] == last
        total += jnp.where(same, piece_ref[j].astype(F32), 0.0)
    total_ref[...] = total


def prefix_kernel(doc_ref, piece_ref, carry_ref, before_ref):
    row, docs = row_docs(doc_ref)
    past = doc_row(doc_ref, jnp.maximum(2 * ROW * row - 1, 0))
    before = jnp.broadcast_to(past[:, BLK - 1 :], (1, HD))
    running = carry_ref[...]
    for j in range(ROW):
        before_ref[j] = running.astype(BF16)
        now = docs[2 * j + 1 : 2 * j + 2, :]
        running = jnp.where(now == before, running, 0.0) + piece_ref[j].astype(F32)
        before = now


def inside_kernel(doc_ref, q_ref, k_ref, v_ref, intra_ref, update_ref):
    me = lax.axis_index("ctx")
    lane = lax.broadcasted_iota(jnp.int32, (BLK, BLK), 1)
    line = lax.broadcasted_iota(jnp.int32, (BLK, BLK), 0)
    causal = lane <= line
    docs = [doc_row(doc_ref, 2 * me), doc_row(doc_ref, 2 * me + 1)]
    cols = [down(docs[0]), down(docs[1])]
    keep = cols[0] == docs[0][:, BLK - 1 :]
    for h in range(4):
        for t in range(2):
            rows = slice(t * BLK, (t + 1) * BLK)
            q, k, v = q_ref[rows, head(h)], k_ref[rows, head(h)], v_ref[rows, head(h)]
            scores = jnp.where(causal & (cols[t] == docs[t]), dot_nt(q, k), 0.0).astype(BF16)
            intra_ref[rows, head(h)] = dot_nn(scores, v)
            if t == 0:
                kept = jnp.where(keep, v.astype(F32), 0.0).astype(BF16)
                update_ref[head(h), :] = dot_tn(k, kept)


def linear_kernel(doc_ref, q_ref, intra_ref, update_ref, state_ref, lin_ref, sq_ref):
    me = lax.axis_index("ctx")
    past = doc_row(doc_ref, jnp.maximum(2 * me - 1, 0))[:, BLK - 1 :]
    docs = [doc_row(doc_ref, 2 * me), doc_row(doc_ref, 2 * me + 1)]
    mid = docs[0][:, BLK - 1 :]
    live = [down(docs[0]) == past, down(docs[1]) == mid]
    squares = [jnp.zeros((BLK, HD), F32), jnp.zeros((BLK, HD), F32)]
    for h in range(4):
        first = state_ref[head(h), :]
        second = (jnp.where(past == mid, first.astype(F32), 0.0) + update_ref[head(h), :]).astype(BF16)
        for t, state in enumerate((first, second)):
            rows = slice(t * BLK, (t + 1) * BLK)
            inner = jnp.where(live[t], dot_nn(q_ref[rows, head(h)], state), 0.0)
            lin = inner + intra_ref[rows, head(h)]
            lin_ref[rows, head(h)] = lin
            squares[t] += lin * lin
    sums = [jnp.sum(square.T, axis=0, keepdims=True) for square in squares]
    row = lax.broadcasted_iota(jnp.int32, (8, BLK), 0)
    tile = jnp.where(row == 0, sums[0], jnp.where(row == 1, sums[1], 0.0))
    for place in range(sq_ref.shape[0]):
        sq_ref[place] = tile


def soft_parts(list_ref, doc_ref, q_ref, kvs, windows, merge):
    me = lax.axis_index("ctx")
    base = 2 * me - NB
    lane = lax.broadcasted_iota(jnp.int32, (BLK, BLK), 1)
    line = lax.broadcasted_iota(jnp.int32, (BLK, BLK), 0)
    causal = lane <= line
    scale = 1.0 / math.sqrt(HD)
    masks = []
    for t in range(2):
        col = down(doc_row(doc_ref, base + NB + t))
        mine = []
        for w in windows:
            if w < t or w > NB + t:
                mine.append(None)
                continue
            block = base + w
            listed = list_ref[t, 0] == block
            for n in range(1, NB):
                listed = listed | (list_ref[t, n] == block)
            listed = listed & (block >= 0)
            row = doc_row(doc_ref, jnp.maximum(block, 0))
            match = col == jnp.where(listed, row, -1.0)
            mine.append(match & causal if w == NB + t else match)
        masks.append(mine)
    for h in range(4):
        q = q_ref[:, head(h)]
        raw = [dot_nt(q, kv[: 2 * BLK, head(h)]) for kv in kvs]
        tops, sums, parts = [], [], []
        for t in range(2):
            rows = slice(t * BLK, (t + 1) * BLK)
            pieces = []
            for n, mask in enumerate(masks[t]):
                if mask is None:
                    pieces.append(None)
                else:
                    piece = raw[n // 2][rows, (n % 2) * BLK : (n % 2 + 1) * BLK]
                    pieces.append(jnp.where(mask, piece, NEG))
            live = [piece for piece in pieces if piece is not None]
            top = jnp.max(functools.reduce(jnp.maximum, live), axis=1, keepdims=True)
            top = jnp.maximum(top, merge.top(h, t))
            expos = [None if piece is None else jnp.exp((piece - top) * scale) for piece in pieces]
            total = jnp.sum(sum(e for e in expos if e is not None), axis=1, keepdims=True)
            zero = jnp.zeros((BLK, BLK), BF16)
            parts.append([zero if e is None else e.astype(BF16) for e in expos])
            tops.append(top)
            sums.append(total)
        out = jnp.zeros((2 * BLK, HD), F32)
        for d, kv in enumerate(kvs):
            both = jnp.concatenate(
                [jnp.concatenate(parts[t][2 * d : 2 * d + 2], axis=1) for t in range(2)], axis=0
            )
            out += dot_nn(both, kv[2 * BLK :, head(h)])
        for t in range(2):
            merge.store(h, t, tops[t], sums[t], out[t * BLK : (t + 1) * BLK], scale)


class Near:
    def __init__(self, acc_ref, stat_ref):
        self.acc, self.stat = acc_ref, stat_ref

    def top(self, h, t):
        return NEG

    def store(self, h, t, top, total, out, scale):
        rows = slice(t * BLK, (t + 1) * BLK)
        self.acc[rows, head(h)] = out
        self.stat[rows, h : h + 1] = top
        self.stat[rows, 4 + h : 5 + h] = total


class Far(Near):
    def __init__(self, acc_ref, stat_ref, soft_ref):
        self.acc, self.stat, self.soft = acc_ref, stat_ref, soft_ref

    def top(self, h, t):
        return self.stat[t * BLK : (t + 1) * BLK, h : h + 1]

    def store(self, h, t, top, total, out, scale):
        rows = slice(t * BLK, (t + 1) * BLK)
        fade = jnp.exp((self.top(h, t) - top) * scale)
        share = 1.0 / (self.stat[rows, 4 + h : 5 + h] * fade + total)
        self.soft[rows, head(h)] = (self.acc[rows, head(h)] * fade + out) * share


def near_kernel(list_ref, doc_ref, q_ref, kv0_ref, kv1_ref, acc_ref, stat_ref):
    soft_parts(list_ref, doc_ref, q_ref, [kv1_ref, kv0_ref], (4, 5, 6, 7), Near(acc_ref, stat_ref))


def far_kernel(list_ref, doc_ref, q_ref, kv2_ref, kv3_ref, acc_ref, stat_ref, soft_ref):
    far = Far(acc_ref, stat_ref, soft_ref)
    soft_parts(list_ref, doc_ref, q_ref, [kv3_ref, kv2_ref], (0, 1, 2, 3), far)


def mix_kernel(lin_ref, soft_ref, sq_ref, gain_ref, out_ref):
    total = jnp.sum(sq_ref[...], axis=0)
    inverse = lax.rsqrt(total / (HEADS * HD) + 1e-06)
    for t in range(2):
        rows = slice(t * BLK, (t + 1) * BLK)
        col = down(inverse[t : t + 1, :])
        for h in range(4):
            normed = lin_ref[rows, head(h)] * col * gain_ref[:, head(h)]
            out_ref[rows, head(h)] = (normed + soft_ref[rows, head(h)]).astype(BF16)


def local(queries, keys, values, doc_ids, key_blocks, norm_gain):
    tok_rows, feat_width = queries.shape
    devices = lax.axis_size("ctx")
    parts = lax.axis_size("dp")
    docs = doc_ids.reshape(-1, BLK)
    gain = norm_gain.reshape(1, feat_width)
    groups = [list(range(first, first + ROW)) for first in range(0, devices, ROW)]
    wide = pltpu.VMEM((tok_rows, feat_width), F32)

    def shifted(x, by):
        return lax.ppermute(x, "ctx", [(i, i + by) for i in range(devices - by)])

    def exchange(x):
        return lax.all_to_all(x, "ctx", 0, 0, axis_index_groups=groups)

    pieces_shape = pltpu.VMEM((ROW, PIECE, HD), BF16)
    summary, kv = call(
        summary_kernel,
        (pltpu.VMEM((ROW * PIECE, HD), BF16), pltpu.VMEM((2 * tok_rows, feat_width), BF16)),
        docs,
        keys,
        values,
    )
    pieces = exchange(summary.reshape(ROW, PIECE, HD))
    kv1 = shifted(kv, 1)
    intra, update = call(
        inside_kernel, (wide, pltpu.VMEM((feat_width, HD), F32)), docs, queries, keys, values
    )
    total = call(total_kernel, pltpu.VMEM((PIECE, HD), F32), docs, pieces)
    carry = shifted(total, ROW)
    kv2 = shifted(kv1, 1)
    before = call(prefix_kernel, pieces_shape, docs, pieces, carry)
    state = exchange(before).reshape(ROW * PIECE, HD)
    kv3 = shifted(kv2, 1)
    near = call(near_kernel, (wide, pltpu.VMEM((tok_rows, HD), F32)), key_blocks, docs, queries, kv, kv1)
    lin, squares = call(
        linear_kernel, (wide, pltpu.VMEM((parts, 8, BLK), F32)), docs, queries, intra, update, state
    )
    squares = lax.all_to_all(squares, "dp", 0, 0)
    soft = call(far_kernel, wide, key_blocks, docs, queries, kv2, kv3, *near)
    return call(
        mix_kernel, jax.ShapeDtypeStruct((tok_rows, feat_width), BF16), lin, soft, squares, gain
    )


def solution(mesh):
    return jax.shard_map(
        local,
        mesh=mesh,
        in_specs=(P("ctx", "dp"), P("ctx", "dp"), P("ctx", "dp"), P(), P("ctx", None), P("dp")),
        out_specs=P("ctx", "dp"),
        check_vma=False,
    )
```

time: 96.1 us -> 89.5 us (0.931)
  blocking collectives: 17.5 us -> 0 us
  waiting for transfers between devices: 35.7 us -> 48 us
  Pallas kernels: 15.9 us -> 10.1 us
  starting transfers between devices: 23.6 us -> 27.9 us
    all_to_all x1 -> x0, blocking collectives: 17.5 us -> none  [exchange(): return lax.all_to_all(x, 'ctx', 0, 0, axis_index_groups=groups)]
    all_to_all x1 -> x2, waiting for transfers between devices: 8.89 us -> 21 us  [exchange(): return lax.all_to_all(x, 'ctx', 0, 0, axis_index_groups=groups)]
    pallas_call x6 -> x8, Pallas kernels: 15.9 us -> 10.1 us  [call(): pl.pallas_call(body, out_shape=outs, in_specs=[SM if small else VM for sm...]
    all_to_all x1 -> x2, starting transfers between devices: 7.42 us -> 11.4 us  [exchange(): return lax.all_to_all(x, 'ctx', 0, 0, axis_index_groups=groups)]
    unnamed x12 -> x18, local copies, waits for them, and re-layouts: 2.67 us -> 2.82 us
  transfers between devices with their start and end apart: 6 -> 7, of which waited for: 5 -> 6; matrix products, arithmetic and copies ran while one was open for 0% -> 0% of each run, Pallas kernels for 12% -> 9%
where the time goes in v2:
time: 89.5 us; the launch traced here: 88.9 us
  waiting for transfers between devices  48 us (54%)
  starting transfers between devices  27.9 us (31%)
  Pallas kernels  10.1 us (11%)
  local copies, waits for them, and re-layouts  2.82 us (3%)
    ppermute x4, waiting for transfers between devices, shifted(): return lax.ppermute(x, 'ctx', [(i, i + by) for i in range(devices - by)])  24.3 us
    all_to_all x2, waiting for transfers between devices, exchange(): return lax.all_to_all(x, 'ctx', 0, 0, axis_index_groups=groups)  21 us
    all_to_all x2, starting transfers between devices, exchange(): return lax.all_to_all(x, 'ctx', 0, 0, axis_index_groups=groups)  11.4 us
    pallas_call x8, Pallas kernels, call(): pl.pallas_call(body, out_shape=outs, in_specs=[SM if small else VM for sm...  10.1 us
    ppermute x4, starting transfers between devices, shifted(): return lax.ppermute(x, 'ctx', [(i, i + by) for i in range(devices - by)])  9.26 us
    all_to_all x1, starting transfers between devices, local(): squares = lax.all_to_all(squares, 'dp', 0, 0)  7.23 us
    unnamed x18, local copies, waits for them, and re-layouts  2.82 us
    all_to_all x1, waiting for transfers between devices, local(): squares = lax.all_to_all(squares, 'dp', 0, 0)  2.63 us
  transfers between devices with their start and end apart: 7, of which 6 were waited for; matrix products, arithmetic and copies ran while one was open for 0% of the time, Pallas kernels for 9%

profile of v2, /device:TPU:2, one launch (start us, length us, event | category | flops | bytes accessed | tf_op | source)
XLA Modules:
  0.0 88.9 jit_solution(11891360008960402007)
XLA Ops:
  0.0 0.0 copy-start
  0.0 0.9 %copy-done = s32[24576]{0:T(1024)S(1)} copy-done((s32[24576]{0:T(1024)S(1)}, s32[24576]{0:T(1024)}, u32[]{:S(2)}) %copy-start) | copy-done | bytes 98328
  0.9 0.0 copy-start.3
  0.9 0.9 %copy-done.3 = bf16[256,512]{1,0:T(8,128)(2,1)S(1)} copy-done((bf16[256,512]{1,0:T(8,128)(2,1)S(1)}, bf16[256,512]{1,0:T(8,128)(2,1)}, u32[]{:S(2)}) %copy-start.3) | copy-done | bytes 262168
  1.8 0.0 copy-start.5
  1.8 0.9 %copy-done.5 = bf16[256,512]{1,0:T(8,128)(2,1)S(1)} copy-done((bf16[256,512]{1,0:T(8,128)(2,1)S(1)}, bf16[256,512]{1,0:T(8,128)(2,1)}, u32[]{:S(2)}) %copy-start.5) | copy-done | bytes 262168
  2.8 1.0 %shard_map.65 = (bf16[576,128]{1,0:T(8,128)(2,1)}, bf16[512,512]{1,0:T(8,128)(2,1)S(1)}) custom-call(s32[192,128]{1,0:T(8,128)S(1)} %bitcast.4, bf16[256,512]{1,0:T(8,128)(2,1)S(1)} %copy-done.3, bf16[256,512]{1,0:T(8,128)(2,1)S(1)} %copy-done.5), custom_call_target="tpu_custom_call" | custom-call | tf_op jit(solution)/shard_map/pallas_call | solution.py:31
  3.8 1.9 %collective-permute-start.1 = (bf16[512,512]{1,0:T(8,128)(2,1)S(1)}, bf16[512,512]{1,0:T(8,128)(2,1)S(1)}, u32[]{:S(2)}, u32[]{:S(2)}) collective-permute-start(bf16[512,512]{1,0:T(8,128)(2,1)S(1)} %get-tuple-element.17.kv0_ref), channel_id=1, source_target_pairs={{0,8},{8,16},{16,24},{24,32},{32,40},{40,48},{48,56},{56,64},{64,7... | collective-permute-start | bytes 1572872 | tf_op jit(solution)/shard_map/ppermute | solution.py:267
  5.8 18.9 %collective-permute-done.1.kv1_ref = bf16[512,512]{1,0:T(8,128)(2,1)S(1)} collective-permute-done((bf16[512,512]{1,0:T(8,128)(2,1)S(1)}, bf16[512,512]{1,0:T(8,128)(2,1)S(1)}, u32[]{:S(2)}, u32[]{:S(2)}) %collective-permute-start.1) | collective-permute-done | bytes 524320 | tf_op jit(solution)/shard_map/ppermute | solution.py:267
  24.7 1.9 %collective-permute-start.2 = (bf16[512,512]{1,0:T(8,128)(2,1)S(1)}, bf16[512,512]{1,0:T(8,128)(2,1)}, u32[]{:S(2)}, u32[]{:S(2)}) collective-permute-start(bf16[512,512]{1,0:T(8,128)(2,1)S(1)} %collective-permute-done.1.kv1_ref), channel_id=1, source_target_pairs={{0,8},{8,16},{16,24},{24,32},{32,40},{40,48},{48,56},{56,64},{64,7... | collective-permute-start | bytes 1572872 | tf_op jit(solution)/shard_map/ppermute | solution.py:267
  26.6 0.0 copy-start.1
  26.6 7.6 %all-to-all-start = ((bf16[24,24,128]{2,1,0:T(8,128)(2,1)}), bf16[24,24,128]{2,1,0:T(8,128)(2,1)S(1)}, u32[]{:S(2)}, u32[]{:S(2)}) async-start(bf16[24,24,128]{2,1,0:T(8,128)(2,1)} %bitcast.1), calls=%async_computation | async-start | bytes 294912 | tf_op jit(solution)/shard_map/all_to_all | solution.py:270
  34.2 3.2 %collective-permute-done.2.kv2_ref = bf16[512,512]{1,0:T(8,128)(2,1)} collective-permute-done((bf16[512,512]{1,0:T(8,128)(2,1)S(1)}, bf16[512,512]{1,0:T(8,128)(2,1)}, u32[]{:S(2)}, u32[]{:S(2)}) %collective-permute-start.2) | collective-permute-done | bytes 524320 | tf_op jit(solution)/shard_map/ppermute | solution.py:267
  37.4 1.9 %collective-permute-start.3 = (bf16[512,512]{1,0:T(8,128)(2,1)}, bf16[512,512]{1,0:T(8,128)(2,1)}, u32[]{:S(2)}, u32[]{:S(2)}) collective-permute-start(bf16[512,512]{1,0:T(8,128)(2,1)} %collective-permute-done.2.kv2_ref), channel_id=1, source_target_pairs={{0,8},{8,16},{16,24},{24,32},{32,40},{40,48},{48,56},{56,64},{64,7... | collective-permute-start | bytes 1572872 | tf_op jit(solution)/shard_map/ppermute | solution.py:267
  39.3 8.9 %all-to-all-done.piece_ref = bf16[24,24,128]{2,1,0:T(8,128)(2,1)S(1)} async-done(((bf16[24,24,128]{2,1,0:T(8,128)(2,1)}), bf16[24,24,128]{2,1,0:T(8,128)(2,1)S(1)}, u32[]{:S(2)}, u32[]{:S(2)}) %all-to-all-start) | async-done | bytes 147488 | tf_op jit(solution)/shard_map/all_to_all | solution.py:270
  48.2 0.0 copy-done.1
  48.2 0.0 copy-start.6
  48.2 0.1 shard_map.66
  48.4 0.0 copy-start.2
  48.4 0.0 copy-start.4
  48.4 3.5 %collective-permute-start = (f32[24,128]{1,0:T(8,128)S(1)}, f32[24,128]{1,0:T(8,128)S(1)}, u32[]{:S(2)}, u32[]{:S(2)}) collective-permute-start(f32[24,128]{1,0:T(8,128)S(1)} %shard_map.66), channel_id=1, source_target_pairs={{0,192},{8,200},{16,208},{24,216},{32,224},{40,232},{48,240},{56,2... | collective-permute-start | bytes 36872 | tf_op jit(solution)/shard_map/ppermute | solution.py:267
  51.9 2.2 %collective-permute-done.carry_ref = f32[24,128]{1,0:T(8,128)S(1)} collective-permute-done((f32[24,128]{1,0:T(8,128)S(1)}, f32[24,128]{1,0:T(8,128)S(1)}, u32[]{:S(2)}, u32[]{:S(2)}) %collective-permute-start) | collective-permute-done | bytes 12320 | tf_op jit(solution)/shard_map/ppermute | solution.py:267
  54.1 0.8 shard_map.67
  54.9 3.8 %all-to-all-start.1 = ((bf16[24,24,128]{2,1,0:T(8,128)(2,1)}), bf16[24,24,128]{2,1,0:T(8,128)(2,1)S(1)}, u32[]{:S(2)}, u32[]{:S(2)}) async-start(bf16[24,24,128]{2,1,0:T(8,128)(2,1)} %shard_map.67), calls=%async_computation.1 | async-start | bytes 294912 | tf_op jit(solution)/shard_map/all_to_all | solution.py:270
  58.7 0.0 copy-done.6
  58.8 0.0 copy-done.2
  58.8 0.0 copy-done.4
  58.8 0.9 shard_map.64
  59.7 12.1 %all-to-all-done.1 = bf16[24,24,128]{2,1,0:T(8,128)(2,1)S(1)} async-done(((bf16[24,24,128]{2,1,0:T(8,128)(2,1)}), bf16[24,24,128]{2,1,0:T(8,128)(2,1)S(1)}, u32[]{:S(2)}, u32[]{:S(2)}) %all-to-all-start.1) | async-done | bytes 147488 | tf_op jit(solution)/shard_map/all_to_all | solution.py:270
  71.7 1.0 %shard_map.68 = (f32[256,512]{1,0:T(8,128)S(1)}, f32[8,8,128]{2,1,0:T(8,128)}) custom-call(s32[192,128]{1,0:T(8,128)S(1)} %bitcast.8, bf16[256,512]{1,0:T(8,128)(2,1)S(1)} %copy-done.2, f32[256,512]{1,0:T(8,128)S(1)} %get-tuple-element.13.intra_ref, f32[512,128]{1,0:T(8,128)S(1)} %get-tuple-element.14.update_ref, bf16[576,128]{1,0:T(8,128)(2,1)S(1)} %bitcast.11), custom_call_target="tpu_custom_call" | custom-call | tf_op jit(solution)/shard_map/pallas_call | solution.py:31
  72.8 0.0 copy-start.7
  72.8 7.2 %all-to-all-start.2 = ((f32[8,8,128]{2,1,0:T(8,128)}), f32[8,8,128]{2,1,0:T(8,128)S(1)}, u32[]{:S(2)}, u32[]{:S(2)}) async-start(f32[8,8,128]{2,1,0:T(8,128)} %get-tuple-element.20), calls=%async_computation.2 | async-start | bytes 65536 | tf_op jit(solution)/shard_map/all_to_all | solution.py:295
  80.0 0.0 copy-done.7
  80.0 2.1 %shard_map.69 = (f32[256,512]{1,0:T(8,128)S(1)}, f32[256,128]{1,0:T(8,128)S(1)}) custom-call(s32[2,6]{1,0:T(2,128)S(1)} %copy-done.7, s32[192,128]{1,0:T(8,128)S(1)} %bitcast.9, bf16[256,512]{1,0:T(8,128)(2,1)S(1)} %copy-done.2, bf16[512,512]{1,0:T(8,128)(2,1)S(1)} %get-tuple-element.17.kv0_ref, bf16[512,512]{1,0:T(8,128)(2,1)S(1)} %collective-permute-done.1.kv1_ref), custom_call_target="tpu_custom_call" | custom-call | tf_op jit(solution)/shard_map/pallas_call | solution.py:31
  82.1 0.0 collective-permute-done.3.kv3_ref
  82.1 3.3 %shard_map.70.soft_ref = f32[256,512]{1,0:T(8,128)S(1)} custom-call(s32[2,6]{1,0:T(2,128)S(1)} %copy-done.7, s32[192,128]{1,0:T(8,128)S(1)} %bitcast.10, bf16[256,512]{1,0:T(8,128)(2,1)S(1)} %copy-done.2, bf16[512,512]{1,0:T(8,128)(2,1)} %collective-permute-done.2.kv2_ref, bf16[512,512]{1,0:T(8,128)(2,1)} %collective-permute-done.3.kv3_ref, ...), custom_call_target="tpu_custom_call" | custom-call | tf_op jit(solution)/shard_map/pallas_call | solution.py:31
  85.4 0.0 copy-start.8
  85.4 2.6 %all-to-all-done.2.sq_ref = f32[8,8,128]{2,1,0:T(8,128)S(1)} async-done(((f32[8,8,128]{2,1,0:T(8,128)}), f32[8,8,128]{2,1,0:T(8,128)S(1)}, u32[]{:S(2)}, u32[]{:S(2)}) %all-to-all-start.2) | async-done | bytes 32800 | tf_op jit(solution)/shard_map/all_to_all | solution.py:295
  88.0 0.0 copy-done.8
  88.0 0.9 shard_map.71
Async XLA Ops:
  0.0 0.9 %copy-start = (s32[24576]{0:T(1024)S(1)}, s32[24576]{0:T(1024)}, u32[]{:S(2)}) copy-start(s32[24576]{0:T(1024)} %param.9) | copy-start | bytes 294916
  0.9 0.9 %copy-start.3 = (bf16[256,512]{1,0:T(8,128)(2,1)S(1)}, bf16[256,512]{1,0:T(8,128)(2,1)}, u32[]{:S(2)}) copy-start(bf16[256,512]{1,0:T(8,128)(2,1)} %k_ref.3) | copy-start | bytes 786436
  1.8 0.9 %copy-start.5 = (bf16[256,512]{1,0:T(8,128)(2,1)S(1)}, bf16[256,512]{1,0:T(8,128)(2,1)}, u32[]{:S(2)}) copy-start(bf16[256,512]{1,0:T(8,128)(2,1)} %v_ref.3) | copy-start | bytes 786436
  3.8 20.8 %collective-permute-start.1 = (bf16[512,512]{1,0:T(8,128)(2,1)S(1)}, bf16[512,512]{1,0:T(8,128)(2,1)S(1)}, u32[]{:S(2)}, u32[]{:S(2)}) collective-permute-start(bf16[512,512]{1,0:T(8,128)(2,1)S(1)} %get-tuple-element.17.kv0_ref), channel_id=1, source_target_pairs={{0,8},{8,16},{16,24},{24,32},{32,40},{40,48},{48,56},{56,64},{64,7... | collective-permute-start | bytes 1572872 | tf_op jit(solution)/shard_map/ppermute | solution.py:267
  24.7 12.7 %collective-permute-start.2 = (bf16[512,512]{1,0:T(8,128)(2,1)S(1)}, bf16[512,512]{1,0:T(8,128)(2,1)}, u32[]{:S(2)}, u32[]{:S(2)}) collective-permute-start(bf16[512,512]{1,0:T(8,128)(2,1)S(1)} %collective-permute-done.1.kv1_ref), channel_id=1, source_target_pairs={{0,8},{8,16},{16,24},{24,32},{32,40},{40,48},{48,56},{56,64},{64,7... | collective-permute-start | bytes 1572872 | tf_op jit(solution)/shard_map/ppermute | solution.py:267
  26.6 21.6 %copy-start.1 = (s32[24576]{0:T(1024)S(1)}, s32[24576]{0:T(1024)}, u32[]{:S(2)}) copy-start(s32[24576]{0:T(1024)} %param.9) | copy-start | bytes 294916
  26.6 21.6 %all-to-all-start = ((bf16[24,24,128]{2,1,0:T(8,128)(2,1)}), bf16[24,24,128]{2,1,0:T(8,128)(2,1)S(1)}, u32[]{:S(2)}, u32[]{:S(2)}) async-start(bf16[24,24,128]{2,1,0:T(8,128)(2,1)} %bitcast.1), calls=%async_computation | async-start | bytes 294912 | tf_op jit(solution)/shard_map/all_to_all | solution.py:270
  37.4 44.7 %collective-permute-start.3 = (bf16[512,512]{1,0:T(8,128)(2,1)}, bf16[512,512]{1,0:T(8,128)(2,1)}, u32[]{:S(2)}, u32[]{:S(2)}) collective-permute-start(bf16[512,512]{1,0:T(8,128)(2,1)} %collective-permute-done.2.kv2_ref), channel_id=1, source_target_pairs={{0,8},{8,16},{16,24},{24,32},{32,40},{40,48},{48,56},{56,64},{64,7... | collective-permute-start | bytes 1572872 | tf_op jit(solution)/shard_map/ppermute | solution.py:267
  48.2 10.5 %copy-start.6 = (bf16[256,512]{1,0:T(8,128)(2,1)S(1)}, bf16[256,512]{1,0:T(8,128)(2,1)}, u32[]{:S(2)}) copy-start(bf16[256,512]{1,0:T(8,128)(2,1)} %v_ref.3) | copy-start | bytes 786436
  48.4 10.4 %copy-start.2 = (bf16[256,512]{1,0:T(8,128)(2,1)S(1)}, bf16[256,512]{1,0:T(8,128)(2,1)}, u32[]{:S(2)}) copy-start(bf16[256,512]{1,0:T(8,128)(2,1)} %q_ref.7) | copy-start | bytes 786436
  48.4 10.4 %copy-start.4 = (bf16[256,512]{1,0:T(8,128)(2,1)S(1)}, bf16[256,512]{1,0:T(8,128)(2,1)}, u32[]{:S(2)}) copy-start(bf16[256,512]{1,0:T(8,128)(2,1)} %k_ref.3) | copy-start | bytes 786436
  48.4 5.7 %collective-permute-start = (f32[24,128]{1,0:T(8,128)S(1)}, f32[24,128]{1,0:T(8,128)S(1)}, u32[]{:S(2)}, u32[]{:S(2)}) collective-permute-start(f32[24,128]{1,0:T(8,128)S(1)} %shard_map.66), channel_id=1, source_target_pairs={{0,192},{8,200},{16,208},{24,216},{32,224},{40,232},{48,240},{56,2... | collective-permute-start | bytes 36872 | tf_op jit(solution)/shard_map/ppermute | solution.py:267
  54.9 16.8 %all-to-all-start.1 = ((bf16[24,24,128]{2,1,0:T(8,128)(2,1)}), bf16[24,24,128]{2,1,0:T(8,128)(2,1)S(1)}, u32[]{:S(2)}, u32[]{:S(2)}) async-start(bf16[24,24,128]{2,1,0:T(8,128)(2,1)} %shard_map.67), calls=%async_computation.1 | async-start | bytes 294912 | tf_op jit(solution)/shard_map/all_to_all | solution.py:270
  72.8 7.2 %copy-start.7 = (s32[2,6]{1,0:T(2,128)S(1)}, s32[2,6]{1,0:T(2,128)}, u32[]{:S(2)}) copy-start(s32[2,6]{1,0:T(2,128)} %list_ref.3) | copy-start | bytes 148
  72.8 15.3 %all-to-all-start.2 = ((f32[8,8,128]{2,1,0:T(8,128)}), f32[8,8,128]{2,1,0:T(8,128)S(1)}, u32[]{:S(2)}, u32[]{:S(2)}) async-start(f32[8,8,128]{2,1,0:T(8,128)} %get-tuple-element.20), calls=%async_computation.2 | async-start | bytes 65536 | tf_op jit(solution)/shard_map/all_to_all | solution.py:295
  85.4 2.6 %copy-start.8 = (f32[512]{0:T(512)S(1)}, f32[512]{0:T(512)}, u32[]{:S(2)}) copy-start(f32[512]{0:T(512)} %param.11) | copy-start | bytes 6148

commit v3 on v2

--- a/solution.py
+++ b/solution.py
@@ -22,17 +22,24 @@
 SM = pl.BlockSpec(memory_space=pltpu.SMEM)
 
 
-def call(body, outs, *operands):
-    smem = [x.shape == (2, NB) for x in operands]
-    operands = [
-        x if small else pltpu.with_memory_space_constraint(x, pltpu.VMEM)
-        for x, small in zip(operands, smem)
-    ]
+def call(body, outs, *operands, scratch=None, aliases=None):
+    small = [x.shape == (2, NB) for x in operands]
+    if scratch is not None:
+        specs = [pl.BlockSpec(memory_space=pltpu.HBM)] * len(operands)
+        operands = [pltpu.with_memory_space_constraint(x, pltpu.HBM) for x in operands]
+    else:
+        specs = [SM if flag else VM for flag in small]
+        operands = [
+            x if flag else pltpu.with_memory_space_constraint(x, pltpu.VMEM)
+            for x, flag in zip(operands, small)
+        ]
     return pl.pallas_call(
         body,
         out_shape=outs,
-        in_specs=[SM if small else VM for small in smem],
+        in_specs=specs,
         out_specs=jax.tree.map(lambda _: VM, outs),
+        scratch_shapes=scratch or (),
+        input_output_aliases=aliases or {},
         compiler_params=pltpu.CompilerParams(vmem_limit_bytes=12 << 20),
     )(*operands)
 
@@ -65,19 +72,29 @@
     return slice(h * HD, (h + 1) * HD)
 
 
-def summary_kernel(doc_ref, k_ref, v_ref, state_ref, kv_ref):
+def summary_kernel(doc_hbm, k_hbm, v_hbm, state_ref, kv_ref, doc_ref, sems):
     me = lax.axis_index("ctx")
-    d0, d1 = doc_row(doc_ref, 2 * me), doc_row(doc_ref, 2 * me + 1)
+    tok = k_hbm.shape[0]
+    group = pl.multiple_of((2 * me // 8) * 8, 8)
+    copies = [
+        pltpu.make_async_copy(doc_hbm.at[pl.ds(group, 8), :], doc_ref, sems.at[0]),
+        pltpu.make_async_copy(k_hbm, kv_ref.at[:tok], sems.at[1]),
+        pltpu.make_async_copy(v_hbm, kv_ref.at[tok:], sems.at[2]),
+    ]
+    for copy in copies:
+        copy.start()
+    state_ref[4 * HD :, :] = jnp.zeros((ROW * PIECE - 4 * HD, HD), BF16)
+    copies[0].wait()
+    d0, d1 = doc_row(doc_ref, 2 * me - group), doc_row(doc_ref, 2 * me - group + 1)
     last = d1[:, BLK - 1 :]
     first = count_below(d0, last) + count_below(d1, last)
-    rows = lax.broadcasted_iota(jnp.int32, (2 * BLK, HD), 0).astype(F32)
+    rows = lax.broadcasted_iota(jnp.int32, (tok, HD), 0).astype(F32)
     keep = rows >= first
+    copies[1].wait()
+    copies[2].wait()
     for h in range(4):
-        vm = jnp.where(keep, v_ref[:, head(h)].astype(F32), 0.0).astype(BF16)
-        state_ref[head(h), :] = dot_tn(k_ref[:, head(h)], vm).astype(BF16)
-    state_ref[4 * HD :, :] = jnp.zeros((ROW * PIECE - 4 * HD, HD), BF16)
-    kv_ref[: 2 * BLK, :] = k_ref[...]
-    kv_ref[2 * BLK :, :] = v_ref[...]
+        vm = jnp.where(keep, kv_ref[tok:, head(h)].astype(F32), 0.0).astype(BF16)
+        state_ref[head(h), :] = dot_tn(kv_ref[:tok, head(h)], vm).astype(BF16)
 
 
 def row_docs(doc_ref):
@@ -106,25 +123,6 @@
         now = docs[2 * j + 1 : 2 * j + 2, :]
         running = jnp.where(now == before, running, 0.0) + piece_ref[j].astype(F32)
         before = now
-
-
-def inside_kernel(doc_ref, q_ref, k_ref, v_ref, intra_ref, update_ref):
-    me = lax.axis_index("ctx")
-    lane = lax.broadcasted_iota(jnp.int32, (BLK, BLK), 1)
-    line = lax.broadcasted_iota(jnp.int32, (BLK, BLK), 0)
-    causal = lane <= line
-    docs = [doc_row(doc_ref, 2 * me), doc_row(doc_ref, 2 * me + 1)]
-    cols = [down(docs[0]), down(docs[1])]
-    keep = cols[0] == docs[0][:, BLK - 1 :]
-    for h in range(4):
-        for t in range(2):
-            rows = slice(t * BLK, (t + 1) * BLK)
-            q, k, v = q_ref[rows, head(h)], k_ref[rows, head(h)], v_ref[rows, head(h)]
-            scores = jnp.where(causal & (cols[t] == docs[t]), dot_nt(q, k), 0.0).astype(BF16)
-            intra_ref[rows, head(h)] = dot_nn(scores, v)
-            if t == 0:
-                kept = jnp.where(keep, v.astype(F32), 0.0).astype(BF16)
-                update_ref[head(h), :] = dot_tn(k, kept)
 
 
 def linear_kernel(doc_ref, q_ref, intra_ref, update_ref, state_ref, lin_ref, sq_ref):
@@ -150,7 +148,7 @@
         sq_ref[place] = tile
 
 
-def soft_parts(list_ref, doc_ref, q_ref, kvs, windows, merge):
+def soft_parts(list_ref, doc_ref, q_ref, kvs, windows, merge, own=None):
     me = lax.axis_index("ctx")
     base = 2 * me - NB
     lane = lax.broadcasted_iota(jnp.int32, (BLK, BLK), 1)
@@ -176,7 +174,9 @@
         masks.append(mine)
     for h in range(4):
         q = q_ref[:, head(h)]
-        raw = [dot_nt(q, kv[: 2 * BLK, head(h)]) for kv in kvs]
+        raw = [dot_nt(q, k_ref[:, head(h)]) for k_ref, _ in kvs]
+        if own is not None:
+            own(h, raw[0])
         tops, sums, parts = [], [], []
         for t in range(2):
             rows = slice(t * BLK, (t + 1) * BLK)
@@ -197,50 +197,77 @@
             tops.append(top)
             sums.append(total)
         out = jnp.zeros((2 * BLK, HD), F32)
-        for d, kv in enumerate(kvs):
+        for d, (_, v_ref) in enumerate(kvs):
             both = jnp.concatenate(
                 [jnp.concatenate(parts[t][2 * d : 2 * d + 2], axis=1) for t in range(2)], axis=0
             )
-            out += dot_nn(both, kv[2 * BLK :, head(h)])
+            out += dot_nn(both, v_ref[:, head(h)])
         for t in range(2):
             merge.store(h, t, tops[t], sums[t], out[t * BLK : (t + 1) * BLK], scale)
 
 
-class Near:
-    def __init__(self, acc_ref, stat_ref):
-        self.acc, self.stat = acc_ref, stat_ref
+class Merge:
+    def __init__(self, acc_in, stat_in, acc_out, stat_out):
+        self.acc_in, self.stat_in, self.acc_out, self.stat_out = acc_in, stat_in, acc_out, stat_out
 
     def top(self, h, t):
-        return NEG
+        return NEG if self.stat_in is None else self.stat_in[t * BLK : (t + 1) * BLK, h : h + 1]
 
     def store(self, h, t, top, total, out, scale):
         rows = slice(t * BLK, (t + 1) * BLK)
-        self.acc[rows, head(h)] = out
-        self.stat[rows, h : h + 1] = top
-        self.stat[rows, 4 + h : 5 + h] = total
-
-
-class Far(Near):
-    def __init__(self, acc_ref, stat_ref, soft_ref):
-        self.acc, self.stat, self.soft = acc_ref, stat_ref, soft_ref
-
-    def top(self, h, t):
-        return self.stat[t * BLK : (t + 1) * BLK, h : h + 1]
-
-    def store(self, h, t, top, total, out, scale):
-        rows = slice(t * BLK, (t + 1) * BLK)
-        fade = jnp.exp((self.top(h, t) - top) * scale)
-        share = 1.0 / (self.stat[rows, 4 + h : 5 + h] * fade + total)
-        self.soft[rows, head(h)] = (self.acc[rows, head(h)] * fade + out) * share
-
-
-def near_kernel(list_ref, doc_ref, q_ref, kv0_ref, kv1_ref, acc_ref, stat_ref):
-    soft_parts(list_ref, doc_ref, q_ref, [kv1_ref, kv0_ref], (4, 5, 6, 7), Near(acc_ref, stat_ref))
-
-
-def far_kernel(list_ref, doc_ref, q_ref, kv2_ref, kv3_ref, acc_ref, stat_ref, soft_ref):
-    far = Far(acc_ref, stat_ref, soft_ref)
-    soft_parts(list_ref, doc_ref, q_ref, [kv3_ref, kv2_ref], (0, 1, 2, 3), far)
+        if self.stat_in is not None:
+            fade = jnp.exp((self.top(h, t) - top) * scale)
+            total = self.stat_in[rows, 4 + h : 5 + h] * fade + total
+            out = self.acc_in[rows, head(h)] * fade + out
+        if self.stat_out is None:
+            out = out * (1.0 / total)
+        else:
+            self.stat_out[rows, h : h + 1] = top
+            self.stat_out[rows, 4 + h : 5 + h] = total
+        self.acc_out[rows, head(h)] = out
+
+
+def halves(kv_ref):
+    return kv_ref.at[: 2 * BLK], kv_ref.at[2 * BLK :]
+
+
+def inside_kernel(
+    list_ref, doc_ref, q_ref, k_ref, v_ref, intra_ref, update_ref, acc_ref, stat_ref
+):
+    me = lax.axis_index("ctx")
+    lane = lax.broadcasted_iota(jnp.int32, (BLK, BLK), 1)
+    line = lax.broadcasted_iota(jnp.int32, (BLK, BLK), 0)
+    causal = lane <= line
+    docs = [doc_row(doc_ref, 2 * me), doc_row(doc_ref, 2 * me + 1)]
+    cols = [down(docs[0]), down(docs[1])]
+    same = [causal & (cols[t] == docs[t]) for t in range(2)]
+    keep = cols[0] == docs[0][:, BLK - 1 :]
+
+    def linear(h, raw):
+        for t in range(2):
+            rows = slice(t * BLK, (t + 1) * BLK)
+            v = v_ref[rows, head(h)]
+            scores = jnp.where(same[t], raw[rows, rows], 0.0).astype(BF16)
+            intra_ref[rows, head(h)] = dot_nn(scores, v)
+            if t == 0:
+                kept = jnp.where(keep, v.astype(F32), 0.0).astype(BF16)
+                update_ref[head(h), :] = dot_tn(k_ref[rows, head(h)], kept)
+
+    first = Merge(None, None, acc_ref, stat_ref)
+    soft_parts(list_ref, doc_ref, q_ref, [(k_ref, v_ref)], (6, 7), first, linear)
+
+
+def near_kernel(
+    list_ref, doc_ref, q_ref, kv1_ref, kv2_ref, acc_in, stat_in, acc_ref, stat_ref
+):
+    kvs = [halves(kv2_ref), halves(kv1_ref)]
+    merge = Merge(acc_in, stat_in, acc_ref, stat_ref)
+    soft_parts(list_ref, doc_ref, q_ref, kvs, (2, 3, 4, 5), merge)
+
+
+def far_kernel(list_ref, doc_ref, q_ref, kv3_ref, acc_in, stat_in, soft_ref):
+    merge = Merge(acc_in, stat_in, soft_ref, None)
+    soft_parts(list_ref, doc_ref, q_ref, [halves(kv3_ref)], (0, 1), merge)
 
 
 def mix_kernel(lin_ref, soft_ref, sq_ref, gain_ref, out_ref):
@@ -270,30 +297,47 @@
         return lax.all_to_all(x, "ctx", 0, 0, axis_index_groups=groups)
 
     pieces_shape = pltpu.VMEM((ROW, PIECE, HD), BF16)
+    soft_shape = (wide, pltpu.VMEM((tok_rows, HD), F32))
     summary, kv = call(
         summary_kernel,
         (pltpu.VMEM((ROW * PIECE, HD), BF16), pltpu.VMEM((2 * tok_rows, feat_width), BF16)),
         docs,
         keys,
         values,
-    )
+        scratch=[pltpu.VMEM((8, BLK), jnp.int32), pltpu.SemaphoreType.DMA((3,))],
+    )
+    kv1 = shifted(kv, 1)
     pieces = exchange(summary.reshape(ROW, PIECE, HD))
-    kv1 = shifted(kv, 1)
-    intra, update = call(
-        inside_kernel, (wide, pltpu.VMEM((feat_width, HD), F32)), docs, queries, keys, values
+    kv2 = shifted(kv1, 1)
+    intra, update, *soft = call(
+        inside_kernel,
+        (wide, pltpu.VMEM((feat_width, HD), F32), *soft_shape),
+        key_blocks,
+        docs,
+        queries,
+        keys,
+        values,
     )
     total = call(total_kernel, pltpu.VMEM((PIECE, HD), F32), docs, pieces)
     carry = shifted(total, ROW)
-    kv2 = shifted(kv1, 1)
     before = call(prefix_kernel, pieces_shape, docs, pieces, carry)
     state = exchange(before).reshape(ROW * PIECE, HD)
     kv3 = shifted(kv2, 1)
-    near = call(near_kernel, (wide, pltpu.VMEM((tok_rows, HD), F32)), key_blocks, docs, queries, kv, kv1)
+    soft = call(
+        near_kernel, soft_shape, key_blocks, docs, queries, kv1, kv2, *soft, aliases={5: 0, 6: 1}
+    )
     lin, squares = call(
-        linear_kernel, (wide, pltpu.VMEM((parts, 8, BLK), F32)), docs, queries, intra, update, state
+        linear_kernel,
+        (wide, pltpu.VMEM((parts, 8, BLK), F32)),
+        docs,
+        queries,
+        intra,
+        update,
+        state,
+        aliases={2: 0},
     )
     squares = lax.all_to_all(squares, "dp", 0, 0)
-    soft = call(far_kernel, wide, key_blocks, docs, queries, kv2, kv3, *near)
+    soft = call(far_kernel, wide, key_blocks, docs, queries, kv3, *soft, aliases={4: 0})
     return call(
         mix_kernel, jax.ShapeDtypeStruct((tok_rows, feat_width), BF16), lin, soft, squares, gain
     )

time: 89.5 us -> 87.6 us (0.979)
  the two profiles are of different devices: /device:TPU:2 before, /device:TPU:4 now
where the time goes in v3:
time: 87.6 us; the launch traced here: 87.1 us
  waiting for transfers between devices  46.4 us (53%)
  starting transfers between devices  27.6 us (32%)
  Pallas kernels  12.9 us (15%)
    ppermute x4, waiting for transfers between devices, shifted(): return lax.ppermute(x, 'ctx', [(i, i + by) for i in range(devices - by)])  24.5 us
    all_to_all x2, waiting for transfers between devices, exchange(): return lax.all_to_all(x, 'ctx', 0, 0, axis_index_groups=groups)  20.4 us
    pallas_call x8, Pallas kernels, call(): pl.pallas_call(body, out_shape=outs, in_specs=specs, out_specs=jax.tree.m...  12.9 us
    all_to_all x2, starting transfers between devices, exchange(): return lax.all_to_all(x, 'ctx', 0, 0, axis_index_groups=groups)  11.5 us
    ppermute x4, starting transfers between devices, shifted(): return lax.ppermute(x, 'ctx', [(i, i + by) for i in range(devices - by)])  8.98 us
    all_to_all x1, starting transfers between devices, local(): squares = lax.all_to_all(squares, 'dp', 0, 0)  7.11 us
  transfers between devices with their start and end apart: 7, of which 6 were waited for; matrix products, arithmetic and copies ran while one was open for 0% of the time, Pallas kernels for 12%

profile of v3, /device:TPU:4, one launch (start us, length us, event | category | flops | bytes accessed | tf_op | source)
XLA Modules:
  0.0 87.1 jit_solution(8659500202414133651)
XLA Ops:
  0.0 2.0 %shard_map.65 = (bf16[576,128]{1,0:T(8,128)(2,1)}, bf16[512,512]{1,0:T(8,128)(2,1)S(1)}) custom-call(s32[192,128]{1,0:T(8,128)} %bitcast.4, bf16[256,512]{1,0:T(8,128)(2,1)} %k_hbm.1, bf16[256,512]{1,0:T(8,128)(2,1)} %v_hbm.1), custom_call_target="tpu_custom_call" | custom-call | tf_op jit(solution)/shard_map/pallas_call | solution.py:36
  2.0 1.9 %collective-permute-start.1 = (bf16[512,512]{1,0:T(8,128)(2,1)S(1)}, bf16[512,512]{1,0:T(8,128)(2,1)S(1)}, u32[]{:S(2)}, u32[]{:S(2)}) collective-permute-start(bf16[512,512]{1,0:T(8,128)(2,1)S(1)} %get-tuple-element.19), channel_id=1, source_target_pairs={{0,8},{8,16},{16,24},{24,32},{32,40},{40,48},{48,56},{56,64},{64,7... | collective-permute-start | bytes 1572872 | tf_op jit(solution)/shard_map/ppermute | solution.py:294
  3.9 18.9 %collective-permute-done.1.kv1_ref = bf16[512,512]{1,0:T(8,128)(2,1)S(1)} collective-permute-done((bf16[512,512]{1,0:T(8,128)(2,1)S(1)}, bf16[512,512]{1,0:T(8,128)(2,1)S(1)}, u32[]{:S(2)}, u32[]{:S(2)}) %collective-permute-start.1) | collective-permute-done | bytes 524320 | tf_op jit(solution)/shard_map/ppermute | solution.py:294
  22.9 1.9 %collective-permute-start.2 = (bf16[512,512]{1,0:T(8,128)(2,1)S(1)}, bf16[512,512]{1,0:T(8,128)(2,1)S(1)}, u32[]{:S(2)}, u32[]{:S(2)}) collective-permute-start(bf16[512,512]{1,0:T(8,128)(2,1)S(1)} %collective-permute-done.1.kv1_ref), channel_id=1, source_target_pairs={{0,8},{8,16},{16,24},{24,32},{32,40},{40,48},{48,56},{56,64},{64,7... | collective-permute-start | bytes 1572872 | tf_op jit(solution)/shard_map/ppermute | solution.py:294
  24.8 0.0 copy-start
  24.8 7.6 %all-to-all-start = ((bf16[24,24,128]{2,1,0:T(8,128)(2,1)}), bf16[24,24,128]{2,1,0:T(8,128)(2,1)S(1)}, u32[]{:S(2)}, u32[]{:S(2)}) async-start(bf16[24,24,128]{2,1,0:T(8,128)(2,1)} %bitcast.1), calls=%async_computation | async-start | bytes 294912 | tf_op jit(solution)/shard_map/all_to_all | solution.py:297
  32.4 3.1 %collective-permute-done.2.kv2_ref = bf16[512,512]{1,0:T(8,128)(2,1)S(1)} collective-permute-done((bf16[512,512]{1,0:T(8,128)(2,1)S(1)}, bf16[512,512]{1,0:T(8,128)(2,1)S(1)}, u32[]{:S(2)}, u32[]{:S(2)}) %collective-permute-start.2) | collective-permute-done | bytes 524320 | tf_op jit(solution)/shard_map/ppermute | solution.py:294
  35.5 1.9 %collective-permute-start.3 = (bf16[512,512]{1,0:T(8,128)(2,1)S(1)}, bf16[512,512]{1,0:T(8,128)(2,1)}, u32[]{:S(2)}, u32[]{:S(2)}) collective-permute-start(bf16[512,512]{1,0:T(8,128)(2,1)S(1)} %collective-permute-done.2.kv2_ref), channel_id=1, source_target_pairs={{0,8},{8,16},{16,24},{24,32},{32,40},{40,48},{48,56},{56,64},{64,7... | collective-permute-start | bytes 1572872 | tf_op jit(solution)/shard_map/ppermute | solution.py:294
  37.4 9.0 %all-to-all-done.piece_ref = bf16[24,24,128]{2,1,0:T(8,128)(2,1)S(1)} async-done(((bf16[24,24,128]{2,1,0:T(8,128)(2,1)}), bf16[24,24,128]{2,1,0:T(8,128)(2,1)S(1)}, u32[]{:S(2)}, u32[]{:S(2)}) %all-to-all-start) | async-done | bytes 147488 | tf_op jit(solution)/shard_map/all_to_all | solution.py:297
  46.4 0.0 copy-done
  46.4 0.0 copy-start.3
  46.4 0.1 shard_map.66
  46.6 0.0 copy-start.1
  46.6 0.0 copy-start.2
  46.6 3.2 %collective-permute-start = (f32[24,128]{1,0:T(8,128)S(1)}, f32[24,128]{1,0:T(8,128)S(1)}, u32[]{:S(2)}, u32[]{:S(2)}) collective-permute-start(f32[24,128]{1,0:T(8,128)S(1)} %shard_map.66), channel_id=1, source_target_pairs={{0,192},{8,200},{16,208},{24,216},{32,224},{40,232},{48,240},{56,2... | collective-permute-start | bytes 36872 | tf_op jit(solution)/shard_map/ppermute | solution.py:294
  49.8 2.5 %collective-permute-done.carry_ref = f32[24,128]{1,0:T(8,128)S(1)} collective-permute-done((f32[24,128]{1,0:T(8,128)S(1)}, f32[24,128]{1,0:T(8,128)S(1)}, u32[]{:S(2)}, u32[]{:S(2)}) %collective-permute-start) | collective-permute-done | bytes 12320 | tf_op jit(solution)/shard_map/ppermute | solution.py:294
  52.3 0.8 shard_map.67
  53.1 0.0 copy-start.4
  53.1 4.0 %all-to-all-start.1 = ((bf16[24,24,128]{2,1,0:T(8,128)(2,1)}), bf16[24,24,128]{2,1,0:T(8,128)(2,1)S(1)}, u32[]{:S(2)}, u32[]{:S(2)}) async-start(bf16[24,24,128]{2,1,0:T(8,128)(2,1)} %shard_map.67), calls=%async_computation.1 | async-start | bytes 294912 | tf_op jit(solution)/shard_map/all_to_all | solution.py:297
  57.1 0.0 copy-done.3
  57.1 0.0 copy-done.1
  57.1 0.0 copy-done.2
  57.1 0.0 copy-done.4
  57.1 1.6 %shard_map.64 = (f32[256,512]{1,0:T(8,128)S(1)}, f32[512,128]{1,0:T(8,128)S(1)}, f32[256,512]{1,0:T(8,128)S(1)}, f32[256,128]{1,0:T(8,128)S(1)}) custom-call(s32[2,6]{1,0:T(2,128)S(1)} %copy-done.4, s32[192,128]{1,0:T(8,128)S(1)} %bitcast.7, bf16[256,512]{1,0:T(8,128)(2,1)S(1)} %copy-done.1, bf16[256,512]{1,0:T(8,128)(2,1)S(1)} %copy-done.2, ...), custom_call_target="tpu_custom_call" | custom-call | tf_op jit(solution)/shard_map/pallas_call | solution.py:36
  58.7 11.4 %all-to-all-done.1 = bf16[24,24,128]{2,1,0:T(8,128)(2,1)S(1)} async-done(((bf16[24,24,128]{2,1,0:T(8,128)(2,1)}), bf16[24,24,128]{2,1,0:T(8,128)(2,1)S(1)}, u32[]{:S(2)}, u32[]{:S(2)}) %all-to-all-start.1) | async-done | bytes 147488 | tf_op jit(solution)/shard_map/all_to_all | solution.py:297
  70.0 1.1 %shard_map.68 = (f32[256,512]{1,0:T(8,128)S(1)}, f32[8,8,128]{2,1,0:T(8,128)}) custom-call(s32[192,128]{1,0:T(8,128)S(1)} %bitcast.8, bf16[256,512]{1,0:T(8,128)(2,1)S(1)} %copy-done.1, f32[256,512]{1,0:T(8,128)S(1)} %get-tuple-element.15.intra_ref, f32[512,128]{1,0:T(8,128)S(1)} %get-tuple-element.16.update_ref, ...), custom_call_target="tpu_custom_call", output_to_operand_aliasing={{0}: (2, {})} | custom-call | tf_op jit(solution)/shard_map/pallas_call | solution.py:36
  71.1 7.1 %all-to-all-start.2 = ((f32[8,8,128]{2,1,0:T(8,128)}), f32[8,8,128]{2,1,0:T(8,128)S(1)}, u32[]{:S(2)}, u32[]{:S(2)}) async-start(f32[8,8,128]{2,1,0:T(8,128)} %get-tuple-element.24), calls=%async_computation.2 | async-start | bytes 65536 | tf_op jit(solution)/shard_map/all_to_all | solution.py:339
  78.2 2.7 %shard_map.69 = (f32[256,512]{1,0:T(8,128)S(1)}, f32[256,128]{1,0:T(8,128)S(1)}) custom-call(s32[2,6]{1,0:T(2,128)S(1)} %copy-done.4, s32[192,128]{1,0:T(8,128)S(1)} %bitcast.9, bf16[256,512]{1,0:T(8,128)(2,1)S(1)} %copy-done.1, bf16[512,512]{1,0:T(8,128)(2,1)S(1)} %collective-permute-done.1.kv1_ref, ...), custom_call_target="tpu_custom_call", output_to_operand_aliasing={{0}: (5, {}), {1}: (6, {})} | custom-call | tf_op jit(solution)/shard_map/pallas_call | solution.py:36
  81.0 0.0 collective-permute-done.3.kv3_ref
  81.0 3.7 %shard_map.70.soft_ref = f32[256,512]{1,0:T(8,128)S(1)} custom-call(s32[2,6]{1,0:T(2,128)S(1)} %copy-done.4, s32[192,128]{1,0:T(8,128)S(1)} %bitcast.10, bf16[256,512]{1,0:T(8,128)(2,1)S(1)} %copy-done.1, bf16[512,512]{1,0:T(8,128)(2,1)} %collective-permute-done.3.kv3_ref, f32[256,512]{1,0:T(8,128)S(1)} %get-tuple-element.22.acc_in, ...), custom_call_target="tpu_custom_call", output_to_operand_aliasing={{}: (4, {})} | custom-call | tf_op jit(solution)/shard_map/pallas_call | solution.py:36
  84.7 0.0 copy-start.5
  84.7 1.5 %all-to-all-done.2.sq_ref = f32[8,8,128]{2,1,0:T(8,128)S(1)} async-done(((f32[8,8,128]{2,1,0:T(8,128)}), f32[8,8,128]{2,1,0:T(8,128)S(1)}, u32[]{:S(2)}, u32[]{:S(2)}) %all-to-all-start.2) | async-done | bytes 32800 | tf_op jit(solution)/shard_map/all_to_all | solution.py:339
  86.2 0.0 copy-done.5
  86.2 0.9 shard_map.71
Async XLA Ops:
  2.0 20.9 %collective-permute-start.1 = (bf16[512,512]{1,0:T(8,128)(2,1)S(1)}, bf16[512,512]{1,0:T(8,128)(2,1)S(1)}, u32[]{:S(2)}, u32[]{:S(2)}) collective-permute-start(bf16[512,512]{1,0:T(8,128)(2,1)S(1)} %get-tuple-element.19), channel_id=1, source_target_pairs={{0,8},{8,16},{16,24},{24,32},{32,40},{40,48},{48,56},{56,64},{64,7... | collective-permute-start | bytes 1572872 | tf_op jit(solution)/shard_map/ppermute | solution.py:294
  22.9 12.6 %collective-permute-start.2 = (bf16[512,512]{1,0:T(8,128)(2,1)S(1)}, bf16[512,512]{1,0:T(8,128)(2,1)S(1)}, u32[]{:S(2)}, u32[]{:S(2)}) collective-permute-start(bf16[512,512]{1,0:T(8,128)(2,1)S(1)} %collective-permute-done.1.kv1_ref), channel_id=1, source_target_pairs={{0,8},{8,16},{16,24},{24,32},{32,40},{40,48},{48,56},{56,64},{64,7... | collective-permute-start | bytes 1572872 | tf_op jit(solution)/shard_map/ppermute | solution.py:294
  24.8 21.6 %copy-start = (s32[24576]{0:T(1024)S(1)}, s32[24576]{0:T(1024)}, u32[]{:S(2)}) copy-start(s32[24576]{0:T(1024)} %param.9) | copy-start | bytes 294916
  24.8 21.6 %all-to-all-start = ((bf16[24,24,128]{2,1,0:T(8,128)(2,1)}), bf16[24,24,128]{2,1,0:T(8,128)(2,1)S(1)}, u32[]{:S(2)}, u32[]{:S(2)}) async-start(bf16[24,24,128]{2,1,0:T(8,128)(2,1)} %bitcast.1), calls=%async_computation | async-start | bytes 294912 | tf_op jit(solution)/shard_map/all_to_all | solution.py:297
  35.5 45.5 %collective-permute-start.3 = (bf16[512,512]{1,0:T(8,128)(2,1)S(1)}, bf16[512,512]{1,0:T(8,128)(2,1)}, u32[]{:S(2)}, u32[]{:S(2)}) collective-permute-start(bf16[512,512]{1,0:T(8,128)(2,1)S(1)} %collective-permute-done.2.kv2_ref), channel_id=1, source_target_pairs={{0,8},{8,16},{16,24},{24,32},{32,40},{40,48},{48,56},{56,64},{64,7... | collective-permute-start | bytes 1572872 | tf_op jit(solution)/shard_map/ppermute | solution.py:294
  46.4 10.6 %copy-start.3 = (bf16[256,512]{1,0:T(8,128)(2,1)S(1)}, bf16[256,512]{1,0:T(8,128)(2,1)}, u32[]{:S(2)}) copy-start(bf16[256,512]{1,0:T(8,128)(2,1)} %v_hbm.1) | copy-start | bytes 786436
  46.6 10.5 %copy-start.1 = (bf16[256,512]{1,0:T(8,128)(2,1)S(1)}, bf16[256,512]{1,0:T(8,128)(2,1)}, u32[]{:S(2)}) copy-start(bf16[256,512]{1,0:T(8,128)(2,1)} %q_ref.7) | copy-start | bytes 786436
  46.6 10.5 %copy-start.2 = (bf16[256,512]{1,0:T(8,128)(2,1)S(1)}, bf16[256,512]{1,0:T(8,128)(2,1)}, u32[]{:S(2)}) copy-start(bf16[256,512]{1,0:T(8,128)(2,1)} %k_hbm.1) | copy-start | bytes 786436
  46.6 5.7 %collective-permute-start = (f32[24,128]{1,0:T(8,128)S(1)}, f32[24,128]{1,0:T(8,128)S(1)}, u32[]{:S(2)}, u32[]{:S(2)}) collective-permute-start(f32[24,128]{1,0:T(8,128)S(1)} %shard_map.66), channel_id=1, source_target_pairs={{0,192},{8,200},{16,208},{24,216},{32,224},{40,232},{48,240},{56,2... | collective-permute-start | bytes 36872 | tf_op jit(solution)/shard_map/ppermute | solution.py:294
  53.1 4.0 %copy-start.4 = (s32[2,6]{1,0:T(2,128)S(1)}, s32[2,6]{1,0:T(2,128)}, u32[]{:S(2)}) copy-start(s32[2,6]{1,0:T(2,128)} %list_ref.5) | copy-start | bytes 148
  53.1 17.0 %all-to-all-start.1 = ((bf16[24,24,128]{2,1,0:T(8,128)(2,1)}), bf16[24,24,128]{2,1,0:T(8,128)(2,1)S(1)}, u32[]{:S(2)}, u32[]{:S(2)}) async-start(bf16[24,24,128]{2,1,0:T(8,128)(2,1)} %shard_map.67), calls=%async_computation.1 | async-start | bytes 294912 | tf_op jit(solution)/shard_map/all_to_all | solution.py:297
  71.1 15.1 %all-to-all-start.2 = ((f32[8,8,128]{2,1,0:T(8,128)}), f32[8,8,128]{2,1,0:T(8,128)S(1)}, u32[]{:S(2)}, u32[]{:S(2)}) async-start(f32[8,8,128]{2,1,0:T(8,128)} %get-tuple-element.24), calls=%async_computation.2 | async-start | bytes 65536 | tf_op jit(solution)/shard_map/all_to_all | solution.py:339
  84.7 1.5 %copy-start.5 = (f32[512]{0:T(512)S(1)}, f32[512]{0:T(512)}, u32[]{:S(2)}) copy-start(f32[512]{0:T(512)} %param.11) | copy-start | bytes 6148

commit v4 on v3

--- a/solution.py
+++ b/solution.py
@@ -15,6 +15,7 @@
 NB = 6
 ROW = 24
 PIECE = 24
+FIRST = 12
 NEG = -1e30
 F32 = jnp.float32
 BF16 = jnp.bfloat16
@@ -103,13 +104,17 @@
     return row, jnp.broadcast_to(docs[:, BLK - 1 :], (2 * ROW, HD))
 
 
+def place(j):
+    return (j - FIRST) % ROW
+
+
 def total_kernel(doc_ref, piece_ref, total_ref):
     _, docs = row_docs(doc_ref)
     last = docs[2 * ROW - 1 :, :]
     total = jnp.zeros((PIECE, HD), F32)
     for j in range(ROW):
         same = docs[2 * j + 1 : 2 * j + 2, :] == last
-        total += jnp.where(same, piece_ref[j].astype(F32), 0.0)
+        total += jnp.where(same, piece_ref[place(j)].astype(F32), 0.0)
     total_ref[...] = total
 
 
@@ -119,9 +124,9 @@
     before = jnp.broadcast_to(past[:, BLK - 1 :], (1, HD))
     running = carry_ref[...]
     for j in range(ROW):
-        before_ref[j] = running.astype(BF16)
+        before_ref[place(j)] = running.astype(BF16)
         now = docs[2 * j + 1 : 2 * j + 2, :]
-        running = jnp.where(now == before, running, 0.0) + piece_ref[j].astype(F32)
+        running = jnp.where(now == before, running, 0.0) + piece_ref[place(j)].astype(F32)
         before = now
 
 
@@ -144,8 +149,8 @@
     sums = [jnp.sum(square.T, axis=0, keepdims=True) for square in squares]
     row = lax.broadcasted_iota(jnp.int32, (8, BLK), 0)
     tile = jnp.where(row == 0, sums[0], jnp.where(row == 1, sums[1], 0.0))
-    for place in range(sq_ref.shape[0]):
-        sq_ref[place] = tile
+    for part in range(sq_ref.shape[0]):
+        sq_ref[part] = tile
 
 
 def soft_parts(list_ref, doc_ref, q_ref, kvs, windows, merge, own=None):
@@ -287,7 +292,9 @@
     parts = lax.axis_size("dp")
     docs = doc_ids.reshape(-1, BLK)
     gain = norm_gain.reshape(1, feat_width)
-    groups = [list(range(first, first + ROW)) for first in range(0, devices, ROW)]
+    groups = [
+        [first + (n + FIRST) % ROW for n in range(ROW)] for first in range(0, devices, ROW)
+    ]
     wide = pltpu.VMEM((tok_rows, feat_width), F32)
 
     def shifted(x, by):

time: 87.6 us -> 83.3 us (0.951)
  the two profiles are of different devices: /device:TPU:4 before, /device:TPU:2 now
where the time goes in v4:
time: 83.3 us; the launch traced here: 82.8 us
  starting transfers between devices  37.9 us (45%)
  waiting for transfers between devices  31.7 us (38%)
  Pallas kernels  12.9 us (15%)
    ppermute x4, waiting for transfers between devices, shifted(): return lax.ppermute(x, 'ctx', [(i, i + by) for i in range(devices - by)])  22.3 us
    all_to_all x2, starting transfers between devices, exchange(): return lax.all_to_all(x, 'ctx', 0, 0, axis_index_groups=groups)  21.5 us
    pallas_call x8, Pallas kernels, call(): pl.pallas_call(body, out_shape=outs, in_specs=specs, out_specs=jax.tree.m...  12.9 us
    ppermute x4, starting transfers between devices, shifted(): return lax.ppermute(x, 'ctx', [(i, i + by) for i in range(devices - by)])  9.39 us
    all_to_all x2, waiting for transfers between devices, exchange(): return lax.all_to_all(x, 'ctx', 0, 0, axis_index_groups=groups)  7.88 us
    all_to_all x1, starting transfers between devices, local(): squares = lax.all_to_all(squares, 'dp', 0, 0)  7.1 us
  transfers between devices with their start and end apart: 7, of which 5 were waited for; matrix products, arithmetic and copies ran while one was open for 0% of the time, Pallas kernels for 12%

profile of v4, /device:TPU:2, one launch (start us, length us, event | category | flops | bytes accessed | tf_op | source)
XLA Modules:
  0.0 82.8 jit_solution(15877073887394316428)
XLA Ops:
  0.0 2.0 %shard_map.65 = (bf16[576,128]{1,0:T(8,128)(2,1)}, bf16[512,512]{1,0:T(8,128)(2,1)S(1)}) custom-call(s32[192,128]{1,0:T(8,128)} %bitcast.4, bf16[256,512]{1,0:T(8,128)(2,1)} %k_hbm.1, bf16[256,512]{1,0:T(8,128)(2,1)} %v_hbm.1), custom_call_target="tpu_custom_call" | custom-call | tf_op jit(solution)/shard_map/pallas_call | solution.py:37
  2.0 1.9 %collective-permute-start.1 = (bf16[512,512]{1,0:T(8,128)(2,1)S(1)}, bf16[512,512]{1,0:T(8,128)(2,1)S(1)}, u32[]{:S(2)}, u32[]{:S(2)}) collective-permute-start(bf16[512,512]{1,0:T(8,128)(2,1)S(1)} %get-tuple-element.19), channel_id=1, source_target_pairs={{0,8},{8,16},{16,24},{24,32},{32,40},{40,48},{48,56},{56,64},{64,7... | collective-permute-start | bytes 1572872 | tf_op jit(solution)/shard_map/ppermute | solution.py:301
  3.9 18.9 %collective-permute-done.1.kv1_ref = bf16[512,512]{1,0:T(8,128)(2,1)S(1)} collective-permute-done((bf16[512,512]{1,0:T(8,128)(2,1)S(1)}, bf16[512,512]{1,0:T(8,128)(2,1)S(1)}, u32[]{:S(2)}, u32[]{:S(2)}) %collective-permute-start.1) | collective-permute-done | bytes 524320 | tf_op jit(solution)/shard_map/ppermute | solution.py:301
  22.9 1.9 %collective-permute-start.2 = (bf16[512,512]{1,0:T(8,128)(2,1)S(1)}, bf16[512,512]{1,0:T(8,128)(2,1)S(1)}, u32[]{:S(2)}, u32[]{:S(2)}) collective-permute-start(bf16[512,512]{1,0:T(8,128)(2,1)S(1)} %collective-permute-done.1.kv1_ref), channel_id=1, source_target_pairs={{0,8},{8,16},{16,24},{24,32},{32,40},{40,48},{48,56},{56,64},{64,7... | collective-permute-start | bytes 1572872 | tf_op jit(solution)/shard_map/ppermute | solution.py:301
  24.8 0.0 copy-start
  24.8 11.6 %all-to-all-start = ((bf16[24,24,128]{2,1,0:T(8,128)(2,1)}), bf16[24,24,128]{2,1,0:T(8,128)(2,1)S(1)}, u32[]{:S(2)}, u32[]{:S(2)}) async-start(bf16[24,24,128]{2,1,0:T(8,128)(2,1)} %bitcast.1), calls=%async_computation | async-start | bytes 294912 | tf_op jit(solution)/shard_map/all_to_all | solution.py:304
  36.4 0.0 collective-permute-done.2.kv2_ref
  36.4 2.0 %collective-permute-start.3 = (bf16[512,512]{1,0:T(8,128)(2,1)S(1)}, bf16[512,512]{1,0:T(8,128)(2,1)}, u32[]{:S(2)}, u32[]{:S(2)}) collective-permute-start(bf16[512,512]{1,0:T(8,128)(2,1)S(1)} %collective-permute-done.2.kv2_ref), channel_id=1, source_target_pairs={{0,8},{8,16},{16,24},{24,32},{32,40},{40,48},{48,56},{56,64},{64,7... | collective-permute-start | bytes 1572872 | tf_op jit(solution)/shard_map/ppermute | solution.py:301
  38.5 3.7 %all-to-all-done.piece_ref = bf16[24,24,128]{2,1,0:T(8,128)(2,1)S(1)} async-done(((bf16[24,24,128]{2,1,0:T(8,128)(2,1)}), bf16[24,24,128]{2,1,0:T(8,128)(2,1)S(1)}, u32[]{:S(2)}, u32[]{:S(2)}) %all-to-all-start) | async-done | bytes 147488 | tf_op jit(solution)/shard_map/all_to_all | solution.py:304
  42.2 0.0 copy-done
  42.2 0.0 copy-start.3
  42.2 0.1 shard_map.66
  42.4 0.0 copy-start.1
  42.4 0.0 copy-start.2
  42.4 3.5 %collective-permute-start = (f32[24,128]{1,0:T(8,128)S(1)}, f32[24,128]{1,0:T(8,128)S(1)}, u32[]{:S(2)}, u32[]{:S(2)}) collective-permute-start(f32[24,128]{1,0:T(8,128)S(1)} %shard_map.66), channel_id=1, source_target_pairs={{0,192},{8,200},{16,208},{24,216},{32,224},{40,232},{48,240},{56,2... | collective-permute-start | bytes 36872 | tf_op jit(solution)/shard_map/ppermute | solution.py:301
  45.9 3.4 %collective-permute-done.carry_ref = f32[24,128]{1,0:T(8,128)S(1)} collective-permute-done((f32[24,128]{1,0:T(8,128)S(1)}, f32[24,128]{1,0:T(8,128)S(1)}, u32[]{:S(2)}, u32[]{:S(2)}) %collective-permute-start) | collective-permute-done | bytes 12320 | tf_op jit(solution)/shard_map/ppermute | solution.py:301
  49.3 0.8 shard_map.67
  50.1 0.0 copy-start.4
  50.1 9.8 %all-to-all-start.1 = ((bf16[24,24,128]{2,1,0:T(8,128)(2,1)}), bf16[24,24,128]{2,1,0:T(8,128)(2,1)S(1)}, u32[]{:S(2)}, u32[]{:S(2)}) async-start(bf16[24,24,128]{2,1,0:T(8,128)(2,1)} %shard_map.67), calls=%async_computation.1 | async-start | bytes 294912 | tf_op jit(solution)/shard_map/all_to_all | solution.py:304
  59.9 0.0 copy-done.3
  59.9 0.0 copy-done.1
  60.0 0.0 copy-done.2
  60.0 0.0 copy-done.4
  60.0 1.6 %shard_map.64 = (f32[256,512]{1,0:T(8,128)S(1)}, f32[512,128]{1,0:T(8,128)S(1)}, f32[256,512]{1,0:T(8,128)S(1)}, f32[256,128]{1,0:T(8,128)S(1)}) custom-call(s32[2,6]{1,0:T(2,128)S(1)} %copy-done.4, s32[192,128]{1,0:T(8,128)S(1)} %bitcast.7, bf16[256,512]{1,0:T(8,128)(2,1)S(1)} %copy-done.1, bf16[256,512]{1,0:T(8,128)(2,1)S(1)} %copy-done.2, ...), custom_call_target="tpu_custom_call" | custom-call | tf_op jit(solution)/shard_map/pallas_call | solution.py:37
  61.6 4.2 %all-to-all-done.1 = bf16[24,24,128]{2,1,0:T(8,128)(2,1)S(1)} async-done(((bf16[24,24,128]{2,1,0:T(8,128)(2,1)}), bf16[24,24,128]{2,1,0:T(8,128)(2,1)S(1)}, u32[]{:S(2)}, u32[]{:S(2)}) %all-to-all-start.1) | async-done | bytes 147488 | tf_op jit(solution)/shard_map/all_to_all | solution.py:304
  65.7 1.1 %shard_map.68 = (f32[256,512]{1,0:T(8,128)S(1)}, f32[8,8,128]{2,1,0:T(8,128)}) custom-call(s32[192,128]{1,0:T(8,128)S(1)} %bitcast.8, bf16[256,512]{1,0:T(8,128)(2,1)S(1)} %copy-done.1, f32[256,512]{1,0:T(8,128)S(1)} %get-tuple-element.15.intra_ref, f32[512,128]{1,0:T(8,128)S(1)} %get-tuple-element.16.update_ref, ...), custom_call_target="tpu_custom_call", output_to_operand_aliasing={{0}: (2, {})} | custom-call | tf_op jit(solution)/shard_map/pallas_call | solution.py:37
  66.8 7.1 %all-to-all-start.2 = ((f32[8,8,128]{2,1,0:T(8,128)}), f32[8,8,128]{2,1,0:T(8,128)S(1)}, u32[]{:S(2)}, u32[]{:S(2)}) async-start(f32[8,8,128]{2,1,0:T(8,128)} %get-tuple-element.24), calls=%async_computation.2 | async-start | bytes 65536 | tf_op jit(solution)/shard_map/all_to_all | solution.py:346
  73.9 2.7 %shard_map.69 = (f32[256,512]{1,0:T(8,128)S(1)}, f32[256,128]{1,0:T(8,128)S(1)}) custom-call(s32[2,6]{1,0:T(2,128)S(1)} %copy-done.4, s32[192,128]{1,0:T(8,128)S(1)} %bitcast.9, bf16[256,512]{1,0:T(8,128)(2,1)S(1)} %copy-done.1, bf16[512,512]{1,0:T(8,128)(2,1)S(1)} %collective-permute-done.1.kv1_ref, ...), custom_call_target="tpu_custom_call", output_to_operand_aliasing={{0}: (5, {}), {1}: (6, {})} | custom-call | tf_op jit(solution)/shard_map/pallas_call | solution.py:37
  76.6 0.0 collective-permute-done.3.kv3_ref
  76.6 3.7 %shard_map.70.soft_ref = f32[256,512]{1,0:T(8,128)S(1)} custom-call(s32[2,6]{1,0:T(2,128)S(1)} %copy-done.4, s32[192,128]{1,0:T(8,128)S(1)} %bitcast.10, bf16[256,512]{1,0:T(8,128)(2,1)S(1)} %copy-done.1, bf16[512,512]{1,0:T(8,128)(2,1)} %collective-permute-done.3.kv3_ref, f32[256,512]{1,0:T(8,128)S(1)} %get-tuple-element.22.acc_in, ...), custom_call_target="tpu_custom_call", output_to_operand_aliasing={{}: (4, {})} | custom-call | tf_op jit(solution)/shard_map/pallas_call | solution.py:37
  80.4 0.0 copy-start.5
  80.4 1.5 %all-to-all-done.2.sq_ref = f32[8,8,128]{2,1,0:T(8,128)S(1)} async-done(((f32[8,8,128]{2,1,0:T(8,128)}), f32[8,8,128]{2,1,0:T(8,128)S(1)}, u32[]{:S(2)}, u32[]{:S(2)}) %all-to-all-start.2) | async-done | bytes 32800 | tf_op jit(solution)/shard_map/all_to_all | solution.py:346
  81.9 0.0 copy-done.5
  81.9 0.9 %shard_map.71 = bf16[256,512]{1,0:T(8,128)(2,1)} custom-call(f32[256,512]{1,0:T(8,128)S(1)} %get-tuple-element.18.lin_ref, f32[256,512]{1,0:T(8,128)S(1)} %shard_map.70.soft_ref, f32[8,8,128]{2,1,0:T(8,128)S(1)} %all-to-all-done.2.sq_ref, f32[1,512]{1,0:T(1,128)S(1)} %bitcast.12), custom_call_target="tpu_custom_call" | custom-call | tf_op jit(solution)/shard_map/pallas_call | solution.py:37
Async XLA Ops:
  2.0 20.9 %collective-permute-start.1 = (bf16[512,512]{1,0:T(8,128)(2,1)S(1)}, bf16[512,512]{1,0:T(8,128)(2,1)S(1)}, u32[]{:S(2)}, u32[]{:S(2)}) collective-permute-start(bf16[512,512]{1,0:T(8,128)(2,1)S(1)} %get-tuple-element.19), channel_id=1, source_target_pairs={{0,8},{8,16},{16,24},{24,32},{32,40},{40,48},{48,56},{56,64},{64,7... | collective-permute-start | bytes 1572872 | tf_op jit(solution)/shard_map/ppermute | solution.py:301
  22.9 13.6 %collective-permute-start.2 = (bf16[512,512]{1,0:T(8,128)(2,1)S(1)}, bf16[512,512]{1,0:T(8,128)(2,1)S(1)}, u32[]{:S(2)}, u32[]{:S(2)}) collective-permute-start(bf16[512,512]{1,0:T(8,128)(2,1)S(1)} %collective-permute-done.1.kv1_ref), channel_id=1, source_target_pairs={{0,8},{8,16},{16,24},{24,32},{32,40},{40,48},{48,56},{56,64},{64,7... | collective-permute-start | bytes 1572872 | tf_op jit(solution)/shard_map/ppermute | solution.py:301
  24.8 17.4 %copy-start = (s32[24576]{0:T(1024)S(1)}, s32[24576]{0:T(1024)}, u32[]{:S(2)}) copy-start(s32[24576]{0:T(1024)} %param.9) | copy-start | bytes 294916
  24.8 17.4 %all-to-all-start = ((bf16[24,24,128]{2,1,0:T(8,128)(2,1)}), bf16[24,24,128]{2,1,0:T(8,128)(2,1)S(1)}, u32[]{:S(2)}, u32[]{:S(2)}) async-start(bf16[24,24,128]{2,1,0:T(8,128)(2,1)} %bitcast.1), calls=%async_computation | async-start | bytes 294912 | tf_op jit(solution)/shard_map/all_to_all | solution.py:304
  36.4 40.2 %collective-permute-start.3 = (bf16[512,512]{1,0:T(8,128)(2,1)S(1)}, bf16[512,512]{1,0:T(8,128)(2,1)}, u32[]{:S(2)}, u32[]{:S(2)}) collective-permute-start(bf16[512,512]{1,0:T(8,128)(2,1)S(1)} %collective-permute-done.2.kv2_ref), channel_id=1, source_target_pairs={{0,8},{8,16},{16,24},{24,32},{32,40},{40,48},{48,56},{56,64},{64,7... | collective-permute-start | bytes 1572872 | tf_op jit(solution)/shard_map/ppermute | solution.py:301
  42.2 17.7 %copy-start.3 = (bf16[256,512]{1,0:T(8,128)(2,1)S(1)}, bf16[256,512]{1,0:T(8,128)(2,1)}, u32[]{:S(2)}) copy-start(bf16[256,512]{1,0:T(8,128)(2,1)} %v_hbm.1) | copy-start | bytes 786436
  42.4 17.6 %copy-start.1 = (bf16[256,512]{1,0:T(8,128)(2,1)S(1)}, bf16[256,512]{1,0:T(8,128)(2,1)}, u32[]{:S(2)}) copy-start(bf16[256,512]{1,0:T(8,128)(2,1)} %q_ref.7) | copy-start | bytes 786436
  42.4 17.6 %copy-start.2 = (bf16[256,512]{1,0:T(8,128)(2,1)S(1)}, bf16[256,512]{1,0:T(8,128)(2,1)}, u32[]{:S(2)}) copy-start(bf16[256,512]{1,0:T(8,128)(2,1)} %k_hbm.1) | copy-start | bytes 786436
  42.4 6.9 %collective-permute-start = (f32[24,128]{1,0:T(8,128)S(1)}, f32[24,128]{1,0:T(8,128)S(1)}, u32[]{:S(2)}, u32[]{:S(2)}) collective-permute-start(f32[24,128]{1,0:T(8,128)S(1)} %shard_map.66), channel_id=1, source_target_pairs={{0,192},{8,200},{16,208},{24,216},{32,224},{40,232},{48,240},{56,2... | collective-permute-start | bytes 36872 | tf_op jit(solution)/shard_map/ppermute | solution.py:301
  50.1 9.9 %copy-start.4 = (s32[2,6]{1,0:T(2,128)S(1)}, s32[2,6]{1,0:T(2,128)}, u32[]{:S(2)}) copy-start(s32[2,6]{1,0:T(2,128)} %list_ref.5) | copy-start | bytes 148
  50.1 15.6 %all-to-all-start.1 = ((bf16[24,24,128]{2,1,0:T(8,128)(2,1)}), bf16[24,24,128]{2,1,0:T(8,128)(2,1)S(1)}, u32[]{:S(2)}, u32[]{:S(2)}) async-start(bf16[24,24,128]{2,1,0:T(8,128)(2,1)} %shard_map.67), calls=%async_computation.1 | async-start | bytes 294912 | tf_op jit(solution)/shard_map/all_to_all | solution.py:304
  66.8 15.1 %all-to-all-start.2 = ((f32[8,8,128]{2,1,0:T(8,128)}), f32[8,8,128]{2,1,0:T(8,128)S(1)}, u32[]{:S(2)}, u32[]{:S(2)}) async-start(f32[8,8,128]{2,1,0:T(8,128)} %get-tuple-element.24), calls=%async_computation.2 | async-start | bytes 65536 | tf_op jit(solution)/shard_map/all_to_all | solution.py:346
  80.4 1.5 %copy-start.5 = (f32[512]{0:T(512)S(1)}, f32[512]{0:T(512)}, u32[]{:S(2)}) copy-start(f32[512]{0:T(512)} %param.11) | copy-start | bytes 6148

commit v5 on v4

--- a/solution.py
+++ b/solution.py
@@ -15,7 +15,8 @@
 NB = 6
 ROW = 24
 PIECE = 24
-FIRST = 12
+FIRST = 15
+LEAD = 6
 NEG = -1e30
 F32 = jnp.float32
 BF16 = jnp.bfloat16
@@ -343,7 +344,8 @@
         state,
         aliases={2: 0},
     )
-    squares = lax.all_to_all(squares, "dp", 0, 0)
+    order = [[(LEAD + n) % parts for n in range(parts)]]
+    squares = lax.all_to_all(squares, "dp", 0, 0, axis_index_groups=order)
     soft = call(far_kernel, wide, key_blocks, docs, queries, kv3, *soft, aliases={4: 0})
     return call(
         mix_kernel, jax.ShapeDtypeStruct((tok_rows, feat_width), BF16), lin, soft, squares, gain

time: 83.3 us -> 82.2 us (0.987)
  the two profiles are of different devices: /device:TPU:2 before, /device:TPU:1 now
where the time goes in v5:
time: 82.2 us; the launch traced here: 81.7 us
  starting transfers between devices  51.2 us (62%)
  waiting for transfers between devices  16.8 us (20%)
  Pallas kernels  12.9 us (16%)
    all_to_all x2, starting transfers between devices, exchange(): return lax.all_to_all(x, 'ctx', 0, 0, axis_index_groups=groups)  29.9 us
    ppermute x4, starting transfers between devices, shifted(): return lax.ppermute(x, 'ctx', [(i, i + by) for i in range(devices - by)])  14.1 us
    pallas_call x8, Pallas kernels, call(): pl.pallas_call(body, out_shape=outs, in_specs=specs, out_specs=jax.tree.m...  12.9 us
    ppermute x4, waiting for transfers between devices, shifted(): return lax.ppermute(x, 'ctx', [(i, i + by) for i in range(devices - by)])  8.59 us
    all_to_all x2, waiting for transfers between devices, exchange(): return lax.all_to_all(x, 'ctx', 0, 0, axis_index_groups=groups)  8.19 us
    all_to_all x1, starting transfers between devices, local(): squares = lax.all_to_all(squares, 'dp', 0, 0, axis_index_groups=order)  7.22 us
  transfers between devices with their start and end apart: 7, of which 4 were waited for; matrix products, arithmetic and copies ran while one was open for 0% of the time, Pallas kernels for 12%

profile of v5, /device:TPU:1, one launch (start us, length us, event | category | flops | bytes accessed | tf_op | source)
XLA Modules:
  0.0 81.7 jit_solution(12562844343372952065)
XLA Ops:
  0.0 2.0 %shard_map.65 = (bf16[576,128]{1,0:T(8,128)(2,1)}, bf16[512,512]{1,0:T(8,128)(2,1)S(1)}) custom-call(s32[192,128]{1,0:T(8,128)} %bitcast.4, bf16[256,512]{1,0:T(8,128)(2,1)} %k_hbm.1, bf16[256,512]{1,0:T(8,128)(2,1)} %v_hbm.1), custom_call_target="tpu_custom_call" | custom-call | tf_op jit(solution)/shard_map/pallas_call | solution.py:38
  2.0 5.4 %collective-permute-start.1 = (bf16[512,512]{1,0:T(8,128)(2,1)S(1)}, bf16[512,512]{1,0:T(8,128)(2,1)S(1)}, u32[]{:S(2)}, u32[]{:S(2)}) collective-permute-start(bf16[512,512]{1,0:T(8,128)(2,1)S(1)} %get-tuple-element.19), channel_id=1, source_target_pairs={{0,8},{8,16},{16,24},{24,32},{32,40},{40,48},{48,56},{56,64},{64,7... | collective-permute-start | bytes 1572872 | tf_op jit(solution)/shard_map/ppermute | solution.py:302
  7.4 7.8 %collective-permute-done.1.kv1_ref = bf16[512,512]{1,0:T(8,128)(2,1)S(1)} collective-permute-done((bf16[512,512]{1,0:T(8,128)(2,1)S(1)}, bf16[512,512]{1,0:T(8,128)(2,1)S(1)}, u32[]{:S(2)}, u32[]{:S(2)}) %collective-permute-start.1) | collective-permute-done | bytes 524320 | tf_op jit(solution)/shard_map/ppermute | solution.py:302
  15.2 2.7 %collective-permute-start.2 = (bf16[512,512]{1,0:T(8,128)(2,1)S(1)}, bf16[512,512]{1,0:T(8,128)(2,1)S(1)}, u32[]{:S(2)}, u32[]{:S(2)}) collective-permute-start(bf16[512,512]{1,0:T(8,128)(2,1)S(1)} %collective-permute-done.1.kv1_ref), channel_id=1, source_target_pairs={{0,8},{8,16},{16,24},{24,32},{32,40},{40,48},{48,56},{56,64},{64,7... | collective-permute-start | bytes 1572872 | tf_op jit(solution)/shard_map/ppermute | solution.py:302
  17.9 0.0 copy-start
  17.9 18.4 %all-to-all-start = ((bf16[24,24,128]{2,1,0:T(8,128)(2,1)}), bf16[24,24,128]{2,1,0:T(8,128)(2,1)S(1)}, u32[]{:S(2)}, u32[]{:S(2)}) async-start(bf16[24,24,128]{2,1,0:T(8,128)(2,1)} %bitcast.1), calls=%async_computation | async-start | bytes 294912 | tf_op jit(solution)/shard_map/all_to_all | solution.py:305
  36.4 0.0 collective-permute-done.2.kv2_ref
  36.4 2.8 %collective-permute-start.3 = (bf16[512,512]{1,0:T(8,128)(2,1)S(1)}, bf16[512,512]{1,0:T(8,128)(2,1)}, u32[]{:S(2)}, u32[]{:S(2)}) collective-permute-start(bf16[512,512]{1,0:T(8,128)(2,1)S(1)} %collective-permute-done.2.kv2_ref), channel_id=1, source_target_pairs={{0,8},{8,16},{16,24},{24,32},{32,40},{40,48},{48,56},{56,64},{64,7... | collective-permute-start | bytes 1572872 | tf_op jit(solution)/shard_map/ppermute | solution.py:302
  39.1 3.5 %all-to-all-done.piece_ref = bf16[24,24,128]{2,1,0:T(8,128)(2,1)S(1)} async-done(((bf16[24,24,128]{2,1,0:T(8,128)(2,1)}), bf16[24,24,128]{2,1,0:T(8,128)(2,1)S(1)}, u32[]{:S(2)}, u32[]{:S(2)}) %all-to-all-start) | async-done | bytes 147488 | tf_op jit(solution)/shard_map/all_to_all | solution.py:305
  42.7 0.0 copy-done
  42.7 0.0 copy-start.3
  42.7 0.1 shard_map.66
  42.8 0.0 copy-start.1
  42.8 0.0 copy-start.2
  42.8 3.2 %collective-permute-start = (f32[24,128]{1,0:T(8,128)S(1)}, f32[24,128]{1,0:T(8,128)S(1)}, u32[]{:S(2)}, u32[]{:S(2)}) collective-permute-start(f32[24,128]{1,0:T(8,128)S(1)} %shard_map.66), channel_id=1, source_target_pairs={{0,192},{8,200},{16,208},{24,216},{32,224},{40,232},{48,240},{56,2... | collective-permute-start | bytes 36872 | tf_op jit(solution)/shard_map/ppermute | solution.py:302
  46.1 0.8 collective-permute-done.carry_ref
  46.9 0.8 shard_map.67
  47.7 0.0 copy-start.4
  47.7 11.4 %all-to-all-start.1 = ((bf16[24,24,128]{2,1,0:T(8,128)(2,1)}), bf16[24,24,128]{2,1,0:T(8,128)(2,1)S(1)}, u32[]{:S(2)}, u32[]{:S(2)}) async-start(bf16[24,24,128]{2,1,0:T(8,128)(2,1)} %shard_map.67), calls=%async_computation.1 | async-start | bytes 294912 | tf_op jit(solution)/shard_map/all_to_all | solution.py:305
  59.1 0.0 copy-done.3
  59.1 0.0 copy-done.1
  59.1 0.0 copy-done.2
  59.1 0.0 copy-done.4
  59.1 1.6 %shard_map.64 = (f32[256,512]{1,0:T(8,128)S(1)}, f32[512,128]{1,0:T(8,128)S(1)}, f32[256,512]{1,0:T(8,128)S(1)}, f32[256,128]{1,0:T(8,128)S(1)}) custom-call(s32[2,6]{1,0:T(2,128)S(1)} %copy-done.4, s32[192,128]{1,0:T(8,128)S(1)} %bitcast.7, bf16[256,512]{1,0:T(8,128)(2,1)S(1)} %copy-done.1, bf16[256,512]{1,0:T(8,128)(2,1)S(1)} %copy-done.2, ...), custom_call_target="tpu_custom_call" | custom-call | tf_op jit(solution)/shard_map/pallas_call | solution.py:38
  60.7 4.7 %all-to-all-done.1 = bf16[24,24,128]{2,1,0:T(8,128)(2,1)S(1)} async-done(((bf16[24,24,128]{2,1,0:T(8,128)(2,1)}), bf16[24,24,128]{2,1,0:T(8,128)(2,1)S(1)}, u32[]{:S(2)}, u32[]{:S(2)}) %all-to-all-start.1) | async-done | bytes 147488 | tf_op jit(solution)/shard_map/all_to_all | solution.py:305
  65.4 1.1 %shard_map.68 = (f32[256,512]{1,0:T(8,128)S(1)}, f32[8,8,128]{2,1,0:T(8,128)}) custom-call(s32[192,128]{1,0:T(8,128)S(1)} %bitcast.8, bf16[256,512]{1,0:T(8,128)(2,1)S(1)} %copy-done.1, f32[256,512]{1,0:T(8,128)S(1)} %get-tuple-element.15.intra_ref, f32[512,128]{1,0:T(8,128)S(1)} %get-tuple-element.16.update_ref, ...), custom_call_target="tpu_custom_call", output_to_operand_aliasing={{0}: (2, {})} | custom-call | tf_op jit(solution)/shard_map/pallas_call | solution.py:38
  66.5 7.2 %all-to-all-start.2 = ((f32[8,8,128]{2,1,0:T(8,128)}), f32[8,8,128]{2,1,0:T(8,128)S(1)}, u32[]{:S(2)}, u32[]{:S(2)}) async-start(f32[8,8,128]{2,1,0:T(8,128)} %get-tuple-element.24), calls=%async_computation.2 | async-start | bytes 65536 | tf_op jit(solution)/shard_map/all_to_all | solution.py:348
  73.7 2.7 %shard_map.69 = (f32[256,512]{1,0:T(8,128)S(1)}, f32[256,128]{1,0:T(8,128)S(1)}) custom-call(s32[2,6]{1,0:T(2,128)S(1)} %copy-done.4, s32[192,128]{1,0:T(8,128)S(1)} %bitcast.9, bf16[256,512]{1,0:T(8,128)(2,1)S(1)} %copy-done.1, bf16[512,512]{1,0:T(8,128)(2,1)S(1)} %collective-permute-done.1.kv1_ref, ...), custom_call_target="tpu_custom_call", output_to_operand_aliasing={{0}: (5, {}), {1}: (6, {})} | custom-call | tf_op jit(solution)/shard_map/pallas_call | solution.py:38
  76.4 0.0 collective-permute-done.3.kv3_ref
  76.4 3.7 %shard_map.70.soft_ref = f32[256,512]{1,0:T(8,128)S(1)} custom-call(s32[2,6]{1,0:T(2,128)S(1)} %copy-done.4, s32[192,128]{1,0:T(8,128)S(1)} %bitcast.10, bf16[256,512]{1,0:T(8,128)(2,1)S(1)} %copy-done.1, bf16[512,512]{1,0:T(8,128)(2,1)} %collective-permute-done.3.kv3_ref, f32[256,512]{1,0:T(8,128)S(1)} %get-tuple-element.22.acc_in, ...), custom_call_target="tpu_custom_call", output_to_operand_aliasing={{}: (4, {})} | custom-call | tf_op jit(solution)/shard_map/pallas_call | solution.py:38
  80.2 0.0 copy-start.5
  80.2 0.0 all-to-all-done.2.sq_ref
  80.2 0.7 copy-done.5
  80.9 0.9 %shard_map.71 = bf16[256,512]{1,0:T(8,128)(2,1)} custom-call(f32[256,512]{1,0:T(8,128)S(1)} %get-tuple-element.18.lin_ref, f32[256,512]{1,0:T(8,128)S(1)} %shard_map.70.soft_ref, f32[8,8,128]{2,1,0:T(8,128)S(1)} %all-to-all-done.2.sq_ref, f32[1,512]{1,0:T(1,128)S(1)} %bitcast.12), custom_call_target="tpu_custom_call" | custom-call | tf_op jit(solution)/shard_map/pallas_call | solution.py:38
Async XLA Ops:
  2.0 13.2 %collective-permute-start.1 = (bf16[512,512]{1,0:T(8,128)(2,1)S(1)}, bf16[512,512]{1,0:T(8,128)(2,1)S(1)}, u32[]{:S(2)}, u32[]{:S(2)}) collective-permute-start(bf16[512,512]{1,0:T(8,128)(2,1)S(1)} %get-tuple-element.19), channel_id=1, source_target_pairs={{0,8},{8,16},{16,24},{24,32},{32,40},{40,48},{48,56},{56,64},{64,7... | collective-permute-start | bytes 1572872 | tf_op jit(solution)/shard_map/ppermute | solution.py:302
  15.2 21.2 %collective-permute-start.2 = (bf16[512,512]{1,0:T(8,128)(2,1)S(1)}, bf16[512,512]{1,0:T(8,128)(2,1)S(1)}, u32[]{:S(2)}, u32[]{:S(2)}) collective-permute-start(bf16[512,512]{1,0:T(8,128)(2,1)S(1)} %collective-permute-done.1.kv1_ref), channel_id=1, source_target_pairs={{0,8},{8,16},{16,24},{24,32},{32,40},{40,48},{48,56},{56,64},{64,7... | collective-permute-start | bytes 1572872 | tf_op jit(solution)/shard_map/ppermute | solution.py:302
  17.9 24.8 %copy-start = (s32[24576]{0:T(1024)S(1)}, s32[24576]{0:T(1024)}, u32[]{:S(2)}) copy-start(s32[24576]{0:T(1024)} %param.9) | copy-start | bytes 294916
  17.9 24.8 %all-to-all-start = ((bf16[24,24,128]{2,1,0:T(8,128)(2,1)}), bf16[24,24,128]{2,1,0:T(8,128)(2,1)S(1)}, u32[]{:S(2)}, u32[]{:S(2)}) async-start(bf16[24,24,128]{2,1,0:T(8,128)(2,1)} %bitcast.1), calls=%async_computation | async-start | bytes 294912 | tf_op jit(solution)/shard_map/all_to_all | solution.py:305
  36.4 40.0 %collective-permute-start.3 = (bf16[512,512]{1,0:T(8,128)(2,1)S(1)}, bf16[512,512]{1,0:T(8,128)(2,1)}, u32[]{:S(2)}, u32[]{:S(2)}) collective-permute-start(bf16[512,512]{1,0:T(8,128)(2,1)S(1)} %collective-permute-done.2.kv2_ref), channel_id=1, source_target_pairs={{0,8},{8,16},{16,24},{24,32},{32,40},{40,48},{48,56},{56,64},{64,7... | collective-permute-start | bytes 1572872 | tf_op jit(solution)/shard_map/ppermute | solution.py:302
  42.7 16.4 %copy-start.3 = (bf16[256,512]{1,0:T(8,128)(2,1)S(1)}, bf16[256,512]{1,0:T(8,128)(2,1)}, u32[]{:S(2)}) copy-start(bf16[256,512]{1,0:T(8,128)(2,1)} %v_hbm.1) | copy-start | bytes 786436
  42.8 16.3 %copy-start.1 = (bf16[256,512]{1,0:T(8,128)(2,1)S(1)}, bf16[256,512]{1,0:T(8,128)(2,1)}, u32[]{:S(2)}) copy-start(bf16[256,512]{1,0:T(8,128)(2,1)} %q_ref.7) | copy-start | bytes 786436
  42.8 16.3 %copy-start.2 = (bf16[256,512]{1,0:T(8,128)(2,1)S(1)}, bf16[256,512]{1,0:T(8,128)(2,1)}, u32[]{:S(2)}) copy-start(bf16[256,512]{1,0:T(8,128)(2,1)} %k_hbm.1) | copy-start | bytes 786436
  42.8 4.1 %collective-permute-start = (f32[24,128]{1,0:T(8,128)S(1)}, f32[24,128]{1,0:T(8,128)S(1)}, u32[]{:S(2)}, u32[]{:S(2)}) collective-permute-start(f32[24,128]{1,0:T(8,128)S(1)} %shard_map.66), channel_id=1, source_target_pairs={{0,192},{8,200},{16,208},{24,216},{32,224},{40,232},{48,240},{56,2... | collective-permute-start | bytes 36872 | tf_op jit(solution)/shard_map/ppermute | solution.py:302
  47.7 11.4 %copy-start.4 = (s32[2,6]{1,0:T(2,128)S(1)}, s32[2,6]{1,0:T(2,128)}, u32[]{:S(2)}) copy-start(s32[2,6]{1,0:T(2,128)} %list_ref.5) | copy-start | bytes 148
  47.7 17.7 %all-to-all-start.1 = ((bf16[24,24,128]{2,1,0:T(8,128)(2,1)}), bf16[24,24,128]{2,1,0:T(8,128)(2,1)S(1)}, u32[]{:S(2)}, u32[]{:S(2)}) async-start(bf16[24,24,128]{2,1,0:T(8,128)(2,1)} %shard_map.67), calls=%async_computation.1 | async-start | bytes 294912 | tf_op jit(solution)/shard_map/all_to_all | solution.py:305
  66.5 13.7 %all-to-all-start.2 = ((f32[8,8,128]{2,1,0:T(8,128)}), f32[8,8,128]{2,1,0:T(8,128)S(1)}, u32[]{:S(2)}, u32[]{:S(2)}) async-start(f32[8,8,128]{2,1,0:T(8,128)} %get-tuple-element.24), calls=%async_computation.2 | async-start | bytes 65536 | tf_op jit(solution)/shard_map/all_to_all | solution.py:348
  80.2 0.7 copy-start.5
